TPU v7x, 32 devices: a whole 2x2x4 slice. The times are simulated.
32 devices in a mesh: seq: 8 (over z, y), tp: 4 (over x, core).
Axes of the slice: x: 2, y: 2, z: 4, core: 2. Of those that a mesh axis runs over, the one named last changes fastest.
Arguments:
- tokens: bfloat16 [16384, 1024], P(('seq', 'tp')), may hold values from -6 to 6
- doc_flags: int32 [16384], P('seq'), may hold values 0 or 1
- reset_flags: int32 [32], P('seq'), may hold values 0 or 1
- state_init: float32 [512, 1024], P(None, 'tp'), may hold values from -6 to 6
- gain_attn: float32 [1024], replicated, may hold values from 0.5 to 1.5
- w_query: bfloat16 [1024, 1024], P(None, 'tp'), may hold values from -0.1875 to 0.1875
- w_key: bfloat16 [1024, 1024], P(None, 'tp'), may hold values from -0.1875 to 0.1875
- w_value: bfloat16 [1024, 1024], P(None, 'tp'), may hold values from -0.1875 to 0.1875
- w_output: bfloat16 [1024, 1024], P('tp'), may hold values from -2 to 2
- bias_table: float32 [8, 32], P('tp'), may hold values from -4 to 4
- state_queries: bfloat16 [512, 1024], P(None, 'tp'), may hold values from -8 to 8
- gate_logits: float32 [1024], P('tp'), may hold values from -1 to 5
- gain_mlp: float32 [1024], replicated, may hold values from 0.5 to 1.5
- w_hidden: bfloat16 [1024, 4096], P(None, 'tp'), may hold values from -0.1875 to 0.1875
- w_return: bfloat16 [4096, 1024], P('tp'), may hold values from -0.09375 to 0.09375
- cotangent: bfloat16 [16384, 1024], P(('seq', 'tp')), may hold values from -6 to 6
Outputs:
- out_tokens: bfloat16 [16384, 1024], P(('seq', 'tp'))
- block_states: float32 [32, 512, 1024], P('seq', None, 'tp')
- grad_tokens: float32 [16384, 1024], P(('seq', 'tp'))
- grad_state: float32 [512, 1024], P('seq', 'tp')
- grad_gain_attn: float32 [1024], replicated
- grad_query: float32 [1024, 1024], P('seq', 'tp')
- grad_key: float32 [1024, 1024], P('seq', 'tp')
- grad_value: float32 [1024, 1024], P('seq', 'tp')
- grad_output: float32 [1024, 1024], P('tp', 'seq')
- grad_bias: float32 [8, 32], replicated
- grad_state_queries: float32 [512, 1024], P('seq', 'tp')
- grad_gate: float32 [1024], replicated
- grad_gain_mlp: float32 [1024], replicated
- grad_hidden: float32 [1024, 4096], P('seq', 'tp')
- grad_return: float32 [4096, 1024], P('tp', 'seq')
Inputs may be any that keep to these rules, and one draw needn't show every extreme that they name: `doc_flags`: 1 marks the first token of a document.
All inputs are finite; a program needn't handle non-finite values. No bound on the sum of `doc_flags` on one device may be relied on, other than what follows from the above.
Results may differ from a plain program's by a relative error of at most 0.02.
Values may be sent and summed in bfloat16 or wider, within the bound.
No kernel may reach another device: no remote copies, remote signals or barrier semaphores. Data moves between devices by JAX's collectives and lax.ppermute only.
A program may use at most 320 MiB of HBM per device.

v0:
```python
import math

import jax
import jax.numpy as jnp
from jax import lax
from jax.sharding import PartitionSpec as P

D = 1024
H = 8
NS = 512
BLOCK = 512
BUCKETS = 32
FAR = 128


eps = 1e-06
negative_fill = -1e30


def from_behind(value, axis, steps):
    count = lax.axis_size(axis)
    leading, last = (max(0, -steps), min(count, count - steps))
    return lax.ppermute(value, axis, [(source, source + steps) for source in range(leading, last)])


def carried_in(shard, axis, combine, identity):
    size, place = (lax.axis_size(axis), lax.axis_index(axis))
    everything = jax.tree.map(lambda part: lax.all_gather(part, axis), shard)
    start = jax.tree.map(
        lambda part, zero: jnp.broadcast_to(jnp.asarray(zero, part.dtype), part.shape),
        shard,
        identity,
    )

    def lap(k, before):
        reached = k < place
        new = combine(before, jax.tree.map(lambda part: part[k], everything))
        return jax.tree.map(lambda a, b: jnp.where(reached, a, b), new, before)

    return lax.fori_loop(0, size, lap, start)


def entering(shard, axis, join, neutral):
    count = lax.axis_size(axis)
    place = lax.axis_index(axis)
    ahead = count - 1 - place
    gathered = jax.tree.map(
        lambda a, kind: lax.all_gather(a.astype(kind), axis), shard, (jnp.bfloat16, jnp.bfloat16)
    )
    state = jax.tree.map(lambda a, e: jnp.zeros_like(a) + jnp.asarray(e, a.dtype), shard, neutral)

    def one(lap, state):
        source = count - 1 - lap
        return join(
            state,
            jax.tree.map(
                lambda a, own: lax.dynamic_index_in_dim(a, source, 0, False).astype(own.dtype),
                gathered,
                shard,
            ),
        )

    return lax.fori_loop(0, ahead, one, state)


def bucket_layout(block):
    rows = lax.broadcasted_iota(jnp.int32, (block, 2 * block), 0)
    columns = lax.broadcasted_iota(jnp.int32, (block, 2 * block), 1)
    distance = block + rows - columns
    clipped = jnp.maximum(distance, 0)
    half = BUCKETS // 2
    limits = [math.ceil(half * (FAR / half) ** (level / half)) for level in range(1, half)]
    extra = sum(((clipped >= limit).astype(jnp.int32) for limit in limits))
    bucket = jnp.where(clipped < half, clipped, half + extra)
    return (distance, bucket)


def rms_scale(values):
    return lax.rsqrt(jnp.mean(values * values, axis=-1, keepdims=True) + eps)


def contract(left, right, left_dim, right_dim):
    return lax.dot_general(
        left, right, (((left_dim,), (right_dim,)), ((), ())), preferred_element_type=jnp.float32
    )


def compose(earlier, later):
    return (later[0] * earlier[0], later[0] * earlier[1] + later[1])


def norm_back(grad_normed, values, inverse, gain):
    scaled = values * inverse
    grad_gain = jnp.sum(grad_normed * scaled, axis=0)
    grad_scaled = grad_normed * gain
    grad_values = inverse * (
        grad_scaled - scaled * jnp.mean(grad_scaled * scaled, axis=-1, keepdims=True)
    )
    return (grad_values, grad_gain)


def gelu_slope(values):
    cumulative = 0.5 * (1.0 + lax.erf(values * (1.0 / math.sqrt(2.0))))
    density = jnp.exp(-0.5 * values * values) * (1.0 / math.sqrt(2.0 * math.pi))
    return cumulative + values * density


def local(
    tokens,
    doc_flags,
    reset_flags,
    state_init,
    gain_attn,
    w_query,
    w_key,
    w_value,
    w_output,
    bias_table,
    state_queries,
    gate_logits,
    gain_mlp,
    w_hidden,
    w_return,
    cotangent,
):
    heads_here = bias_table.shape[0]
    local_width = w_query.shape[1]
    head_size = local_width // heads_here
    width = tokens.shape[1]
    blocks_here = reset_flags.shape[0]
    block = BLOCK
    span = blocks_here * block
    scale = 1.0 / math.sqrt(head_size)
    seq_index = lax.axis_index("seq")
    tp_index = lax.axis_index("tp")
    distance, bucket = bucket_layout(block)
    window_ok = (distance >= 0) & (distance < block)
    bias_window = sum(
        (bias_table[:, slot][:, None, None] * (bucket == slot)[None] for slot in range(BUCKETS))
    )
    bias_joined = jnp.concatenate(
        [bias_window, jnp.zeros((heads_here, block, NS), jnp.float32)], axis=2
    )
    positions = lax.broadcasted_iota(jnp.int32, (2 * block,), 0)
    gates = jax.nn.sigmoid(gate_logits)
    keeps = (1 - reset_flags).astype(jnp.float32)
    query_states = state_queries.reshape(NS, heads_here, head_size)
    token_float = tokens.astype(jnp.float32)
    norm_attn = rms_scale(token_float)
    normed = (token_float * norm_attn * gain_attn).astype(jnp.bfloat16)
    joined_weights = jnp.concatenate([w_query, w_key, w_value], axis=1)
    piece = lax.all_gather(normed, "tp", axis=0, tiled=True)
    project_mixed = jnp.dot(piece, joined_weights, preferred_element_type=jnp.float32).astype(
        jnp.bfloat16
    )
    gathered = jnp.concatenate([piece, project_mixed], axis=1)
    normed_all = gathered[:, :width]
    query_all = gathered[:, width : width + local_width]
    key_all = gathered[:, width + local_width : width + 2 * local_width]
    value_all = gathered[:, width + 2 * local_width :]
    key_prev, value_prev, flag_prev = from_behind(
        (key_all[span - block :], value_all[span - block :], doc_flags[span - block :]), "seq", 1
    )

    def block_heads(array, index):
        return array[index * block : (index + 1) * block].reshape(block, heads_here, head_size)

    def update_probs(index):
        scores = (
            jnp.einsum(
                "nhd,khd->hnk",
                query_states,
                block_heads(key_all, index),
                preferred_element_type=jnp.float32,
            )
            * scale
        )
        return jax.nn.softmax(scores, axis=2)

    updates = []
    factor_total = jnp.ones_like(gates)
    shift_total = jnp.zeros((NS, local_width), jnp.float32)
    for index in range(blocks_here):
        probs = update_probs(index).astype(jnp.bfloat16)
        update = jnp.einsum(
            "hnk,khd->nhd", probs, block_heads(value_all, index), preferred_element_type=jnp.float32
        ).reshape(NS, local_width)
        updates.append(update)
        factor = gates * keeps[index]
        factor_total = factor * factor_total
        shift_total = factor * shift_total + update
    identity = (jnp.ones_like(gates), jnp.zeros_like(shift_total))
    prefix_factor, prefix_shift = carried_in((factor_total, shift_total), "seq", compose, identity)
    state = prefix_factor * state_init + prefix_shift
    used_states = []
    next_states = []
    for index in range(blocks_here):
        used = state * keeps[index]
        used_states.append(used)
        state = gates * used + updates[index]
        next_states.append(state)
    block_states = jnp.stack(next_states)

    def window(index):
        start = index * block
        if index == 0:
            key_before = key_prev
            value_before = value_prev
            flag_before = flag_prev
        else:
            key_before = key_all[start - block : start]
            value_before = value_all[start - block : start]
            flag_before = doc_flags[start - block : start]
        state_low = used_states[index].astype(jnp.bfloat16)
        keys = jnp.concatenate([key_before, key_all[start : start + block], state_low]).reshape(
            2 * block + NS, heads_here, head_size
        )
        values = jnp.concatenate(
            [value_before, value_all[start : start + block], state_low]
        ).reshape(2 * block + NS, heads_here, head_size)
        counts = jnp.cumsum(jnp.concatenate([flag_before, doc_flags[start : start + block]]))
        exists = (positions >= block) | (seq_index * blocks_here + index > 0)
        valid = (counts[block:][:, None] == counts[None, :]) & exists[None, :] & window_ok
        valid = jnp.concatenate([valid, jnp.ones((block, NS), jnp.bool_)], axis=1)
        query = block_heads(query_all, index)
        scores = (
            jnp.einsum("qhd,khd->hqk", query, keys, preferred_element_type=jnp.float32) * scale
            + bias_joined
        )
        scores = jnp.where(valid[None], scores, negative_fill)
        return (query, keys, values, scores)

    outputs = []
    log_totals = []
    for index in range(blocks_here):
        query, keys, values, scores = window(index)
        peak = jnp.max(scores, axis=2, keepdims=True)
        log_total = peak + jnp.log(jnp.sum(jnp.exp(scores - peak), axis=2, keepdims=True))
        probs = jnp.exp(scores - log_total).astype(jnp.bfloat16)
        mixed = jnp.einsum("hqk,khd->qhd", probs, values, preferred_element_type=jnp.float32)
        outputs.append(mixed.reshape(block, local_width))
        log_totals.append(log_total)
    output_low = jnp.concatenate(outputs).astype(jnp.bfloat16)
    attention = lax.psum_scatter(
        jnp.dot(output_low, w_output, preferred_element_type=jnp.float32),
        "tp",
        scatter_dimension=0,
        tiled=True,
    )
    residual = token_float + attention
    norm_mlp = rms_scale(residual)
    normed_mlp = (residual * norm_mlp * gain_mlp).astype(jnp.bfloat16)
    piece = lax.all_gather(normed_mlp, "tp", axis=0, tiled=True)
    hidden = jax.nn.gelu(
        jnp.dot(piece, w_hidden, preferred_element_type=jnp.float32), approximate=False
    ).astype(jnp.bfloat16)
    expanded = jnp.concatenate([piece, hidden], axis=1)
    mlp_inputs = expanded[:, :width]
    activations = expanded[:, width:]
    mlp_out = lax.psum_scatter(
        jnp.dot(activations, w_return, preferred_element_type=jnp.float32).astype(jnp.bfloat16),
        "tp",
        scatter_dimension=0,
        tiled=True,
    ).astype(jnp.float32)
    result = (residual + mlp_out).astype(jnp.bfloat16)
    piece = lax.all_gather(cotangent, "tp", axis=0, tiled=True)
    grad_return_sum = contract(activations, piece, 0, 0)
    pre = jnp.dot(mlp_inputs, w_hidden, preferred_element_type=jnp.float32)
    grad_act = contract(piece, w_return, 1, 1)
    mlp_grad_pre = (grad_act * gelu_slope(pre)).astype(jnp.bfloat16)
    grad_hidden_w = contract(mlp_inputs, mlp_grad_pre, 0, 0)
    grad_normed_mlp = lax.psum_scatter(
        contract(mlp_grad_pre, w_hidden, 1, 1), "tp", scatter_dimension=0, tiled=True
    )
    grad_residual_norm, gain_mlp_part = norm_back(grad_normed_mlp, residual, norm_mlp, gain_mlp)
    grad_residual = cotangent.astype(jnp.float32) + grad_residual_norm
    grad_attn_low = grad_residual.astype(jnp.bfloat16)
    piece = lax.all_gather(grad_attn_low, "tp", axis=0, tiled=True)
    grad_w_sum = contract(output_low, piece, 0, 0)
    output_grad_mixed = contract(piece, w_output, 1, 1).astype(jnp.bfloat16)
    grad_query_blocks = []
    grad_key_blocks = [jnp.zeros((block, local_width), jnp.float32) for index in range(blocks_here)]
    grad_value_blocks = [
        jnp.zeros((block, local_width), jnp.float32) for index in range(blocks_here)
    ]
    direct_grads = []
    bias_grad_sum = jnp.zeros((heads_here, block, 2 * block), jnp.float32)
    halo_key = jnp.zeros((block, local_width), jnp.float32)
    halo_value = jnp.zeros((block, local_width), jnp.float32)
    for index in range(blocks_here):
        query, keys, values, scores = window(index)
        probs_exact = jnp.exp(scores - log_totals[index])
        probs = probs_exact.astype(jnp.bfloat16)
        grad_mixed = block_heads(output_grad_mixed, index)
        grad_probs = jnp.einsum(
            "qhd,khd->hqk", grad_mixed, values, preferred_element_type=jnp.float32
        )
        inner = jnp.sum(probs_exact * grad_probs, axis=2, keepdims=True)
        grad_scores = (probs_exact * (grad_probs - inner)).astype(jnp.bfloat16)
        bias_grad_sum = bias_grad_sum + grad_scores[:, :, : 2 * block].astype(jnp.float32)
        grad_query_blocks.append(
            (
                jnp.einsum("hqk,khd->qhd", grad_scores, keys, preferred_element_type=jnp.float32)
                * scale
            ).reshape(block, local_width)
        )
        grad_keys = (
            jnp.einsum("hqk,qhd->khd", grad_scores, query, preferred_element_type=jnp.float32)
            * scale
        ).reshape(2 * block + NS, local_width)
        grad_values = jnp.einsum(
            "hqk,qhd->khd", probs, grad_mixed, preferred_element_type=jnp.float32
        ).reshape(2 * block + NS, local_width)
        grad_key_blocks[index] = grad_keys[block : 2 * block]
        grad_value_blocks[index] = grad_values[block : 2 * block]
        if index == 0:
            halo_key = grad_keys[:block]
            halo_value = grad_values[:block]
        else:
            grad_key_blocks[index - 1] = grad_key_blocks[index - 1] + grad_keys[:block]
            grad_value_blocks[index - 1] = grad_value_blocks[index - 1] + grad_values[:block]
        direct_grads.append(grad_keys[2 * block :] + grad_values[2 * block :])
    key_back, value_back = (
        from_behind(halo_key.astype(jnp.bfloat16), "seq", -1).astype(halo_key.dtype),
        from_behind(halo_value.astype(jnp.bfloat16), "seq", -1).astype(halo_value.dtype),
    )
    grad_key_blocks[-1] = grad_key_blocks[-1] + key_back
    grad_value_blocks[-1] = grad_value_blocks[-1] + value_back
    carried = jnp.zeros_like(shift_total)
    for index in reversed(range(blocks_here)):
        carried = keeps[index] * (direct_grads[index] + gates * carried)
    local_grad = carried
    incoming = entering((factor_total, local_grad), "seq", compose, identity)[1]
    carried = incoming
    grad_updates = [carried for index in range(blocks_here)]
    gate_sum = jnp.zeros_like(gates)
    for index in reversed(range(blocks_here)):
        grad_updates[index] = carried
        gate_sum = gate_sum + jnp.sum(carried * used_states[index], axis=0)
        carried = keeps[index] * (direct_grads[index] + gates * carried)
    grad_state_part = prefix_factor * local_grad
    grad_state_queries = jnp.zeros((NS, heads_here, head_size), jnp.float32)
    for index in range(blocks_here):
        key_heads = block_heads(key_all, index)
        value_heads = block_heads(value_all, index)
        probs_exact = update_probs(index)
        probs = probs_exact.astype(jnp.bfloat16)
        grad_update = grad_updates[index].astype(jnp.bfloat16).reshape(NS, heads_here, head_size)
        grad_probs = jnp.einsum(
            "nhd,khd->hnk", grad_update, value_heads, preferred_element_type=jnp.float32
        )
        inner = jnp.sum(probs_exact * grad_probs, axis=2, keepdims=True)
        grad_scores = (probs_exact * (grad_probs - inner)).astype(jnp.bfloat16)
        grad_state_queries = (
            grad_state_queries
            + jnp.einsum("hnk,khd->nhd", grad_scores, key_heads, preferred_element_type=jnp.float32)
            * scale
        )
        grad_key_blocks[index] = grad_key_blocks[index] + (
            jnp.einsum(
                "hnk,nhd->khd", grad_scores, query_states, preferred_element_type=jnp.float32
            )
            * scale
        ).reshape(block, local_width)
        grad_value_blocks[index] = grad_value_blocks[index] + jnp.einsum(
            "hnk,nhd->khd", probs, grad_update, preferred_element_type=jnp.float32
        ).reshape(block, local_width)
    grad_joined = jnp.concatenate(
        [
            jnp.concatenate(grad_query_blocks),
            jnp.concatenate(grad_key_blocks),
            jnp.concatenate(grad_value_blocks),
        ],
        axis=1,
    ).astype(jnp.bfloat16)
    grad_weights_joined = contract(normed_all, grad_joined, 0, 0)
    grad_normed = lax.psum_scatter(
        contract(grad_joined, joined_weights, 1, 1).astype(jnp.bfloat16),
        "tp",
        scatter_dimension=0,
        tiled=True,
    ).astype(jnp.float32)
    grad_input_norm, gain_attn_part = norm_back(grad_normed, token_float, norm_attn, gain_attn)
    grad_tokens = grad_residual + grad_input_norm
    bias_local = jnp.stack(
        [
            jnp.sum(jnp.where(bucket == slot, bias_grad_sum, 0.0), axis=(1, 2))
            for slot in range(BUCKETS)
        ],
        axis=1,
    )
    bias_full = lax.dynamic_update_slice(
        jnp.zeros((H, BUCKETS), jnp.float32), bias_local, (tp_index * heads_here, 0)
    )
    gate_full = lax.dynamic_update_slice(
        jnp.zeros((D,), jnp.float32), gate_sum * gates * (1.0 - gates), (tp_index * local_width,)
    )
    grad_gain_attn, grad_gain_mlp, grad_bias, grad_gate = lax.psum(
        (gain_attn_part, gain_mlp_part, bias_full, gate_full), ("seq", "tp")
    )
    queries_flat = grad_state_queries.reshape(NS, local_width)
    joined_sent, output_sent, queries_sent, state_sent, hidden_sent, return_sent = (
        lax.psum_scatter(grad_weights_joined, "seq", scatter_dimension=0, tiled=True),
        lax.psum_scatter(grad_w_sum, "seq", scatter_dimension=1, tiled=True),
        lax.psum_scatter(queries_flat, "seq", scatter_dimension=0, tiled=True),
        lax.psum_scatter(grad_state_part, "seq", scatter_dimension=0, tiled=True),
        lax.psum_scatter(grad_hidden_w, "seq", scatter_dimension=0, tiled=True),
        lax.psum_scatter(grad_return_sum, "seq", scatter_dimension=1, tiled=True),
    )
    grad_query = joined_sent[:, :local_width]
    grad_key = joined_sent[:, local_width : 2 * local_width]
    grad_value = joined_sent[:, 2 * local_width :]
    return (
        result,
        block_states,
        grad_tokens,
        state_sent,
        grad_gain_attn,
        grad_query,
        grad_key,
        grad_value,
        output_sent,
        grad_bias,
        queries_sent,
        grad_gate,
        grad_gain_mlp,
        hidden_sent,
        return_sent,
    )


def solution(mesh):
    return jax.shard_map(
        local,
        mesh=mesh,
        in_specs=(
            P(("seq", "tp"), None),
            P("seq"),
            P("seq"),
            P(None, "tp"),
            P(),
            P(None, "tp"),
            P(None, "tp"),
            P(None, "tp"),
            P("tp", None),
            P("tp", None),
            P(None, "tp"),
            P("tp"),
            P(),
            P(None, "tp"),
            P("tp", None),
            P(("seq", "tp"), None),
        ),
        out_specs=(
            P(("seq", "tp"), None),
            P("seq", None, "tp"),
            P(("seq", "tp"), None),
            P("seq", "tp"),
            P(),
            P("seq", "tp"),
            P("seq", "tp"),
            P("seq", "tp"),
            P("tp", "seq"),
            P(),
            P("seq", "tp"),
            P(),
            P(),
            P("seq", "tp"),
            P("tp", "seq"),
        ),
        check_vma=False,
    )
```

profile of v0, /device:TPU:0, one launch (start us, length us, event | category | flops | bytes accessed | tf_op | source)
XLA Modules:
  0.0 1255.8 jit_solution(14786435407029232076)
XLA Ops:
  12.7 5.4 collective-permute-start.1
  32.3 18.2 %all-gather.2 = f32[8,1,256]{2,1,0:T(1,128)S(1)} all-gather(f32[1,1,256]{2,1,0:T(1,128)S(1)} %bitcast.564), channel_id=2, replica_groups=mesh['seq'=8,'tp'=4] {'seq'}, dimensions={0}, use_global_device_ids=true | all-gather | bytes 9216 | tf_op jit(solution)/shard_map/all_gather | solution.py:28
  53.9 6.1 convolution_convert_fusion.2
  91.9 31.7 %broadcast_compare_fusion.31 = (pred[512,1024]{1,0:T(8,128)(4,1)}, f32[512,1024]{1,0:T(8,128)}, f32[512,1024]{1,0:T(8,128)}, f32[512,1024]{1,0:T(8,128)}, f32[51...) fusion(s32[512]{0:T(512)S(1)} %iota_add_fusion, ...), kind=kLoop, calls=%fused_computation.260 | loop fusion | flops 67108864 | bytes 86013952 | tf_op jit(solution)/shard_map/eq | solution.py:139
  127.0 23.9 %multiply_add_fusion = f32[2,512,1024]{2,1,0:T(8,128)} fusion(f32[512,1024]{1,0:T(8,128)} %get-tuple-element.478, f32[2]{0:T(128)S(1)} %copy-done.166, f32[512,1024]{1,0:T(8,128)} %get-tuple-element.453, f32[2]{0:T(128)S(1)} %copy-done.167, f32[512,1024]{1,0:T(8,128)} %get-tuple-element.454, f32[2]{0:T(128)S(1)} %get-tuple-element.332, ...), kind=kLoop, calls=%fused_computation.98 | loop fusion | flops 66060288 | bytes 71303424 | tf_op jit(solution)/shard_map/add | solution.py:138
  162.4 12.7 %while.31 = (s32[]{:T(128)}, f32[256]{0:T(256)S(1)}, f32[512,256]{1,0:T(8,128)S(1)}, s32[]{:T(128)}, f32[8,256]{1,0:T(8,128)S(1)}, /*index=5*/f32[8,512,256]{2,1,0:T(8,128)}, s32[]{:T(128)}, s32[]{:T(128)}) while((s32[]{:T(128)}, f32[256]{0:T(256)S(1)}, f32[512,256]{1,0:T(8,128)S(1)}, s32[]{:T(128)}, f32[8,256]{1,0:T(8,128)S(1)}, ...), condition=%wide.region_10.11_spmd.clone, body=%wide.region_9.10_spmd.clone.sunk | while | flops 525060 | bytes 1579123 | solution.py:40
  176.1 6.0 bitcast_add_fusion.3
  208.3 4.5 fusion.152
  212.9 75.9 %reduce-scatter.13.cloned.1.call-done = f32[512,1024]{1,0:T(8,128)} async-done(((f32[2048,1024]{1,0:T(8,128)}), f32[512,1024]{1,0:T(8,128)}) %reduce-scatter.13.cloned.1.call-update) | async-done | bytes 2097168 | tf_op jit(solution)/shard_map/reduce_scatter | solution.py:244
  294.0 34.0 %all-gather.15.cloned.1.call-done = bf16[2048,1024]{1,0:T(8,128)(2,1)} async-done(((bf16[512,1024]{1,0:T(8,128)(2,1)}), bf16[2048,1024]{1,0:T(8,128)(2,1)}) %all-gather.15.cloned.1.call-update) | async-done | bytes 4194320 | tf_op jit(solution)/shard_map/all_gather | solution.py:253
  328.0 24.8 %fusion.7 = (bf16[2048,1024]{1,0:T(8,128)(2,1)}, f32[2048,1024]{1,0:T(8,128)}) fusion(bf16[2048,1024]{1,0:T(8,128)(2,1)} %all-gather.15.cloned.1.call-done, bf16[1024,1024]{1,0:T(8,128)(2,1)S(1)} %copy-done), kind=kOutput, calls=%fused_computation.14 | convolution fusion | flops 4431282176 | bytes 18874368 | tf_op jit(solution)/shard_map/dot_general | solution.py:255
  352.8 11.2 all-gather.17.cloned.1.call-done
  364.0 10.2 fusion.13
  376.3 7.0 fusion.215
  383.3 71.8 %reduce-scatter.17.cloned.1.call-done = f32[512,1024]{1,0:T(8,128)} async-done(((f32[2048,1024]{1,0:T(8,128)}), f32[512,1024]{1,0:T(8,128)}) %reduce-scatter.17.cloned.1.call-update) | async-done | bytes 2097168 | tf_op jit(solution)/shard_map/reduce_scatter | solution.py:273
  459.8 34.6 %all-gather.19.cloned.1.call-done = bf16[2048,1024]{1,0:T(8,128)(2,1)} async-done(((bf16[512,1024]{1,0:T(8,128)(2,1)}), bf16[2048,1024]{1,0:T(8,128)(2,1)}) %all-gather.19.cloned.1.call-update) | async-done | bytes 4194320 | tf_op jit(solution)/shard_map/all_gather | solution.py:279
  494.4 3.7 convolution_convert_fusion.3
  498.2 4.2 convolution_bitcast_fusion.1
  505.0 4.2 multiply_reduce_fusion.1
  511.6 4.2 multiply_reduce_fusion.2
  518.3 4.2 multiply_reduce_fusion.3
  529.1 5.4 multiply_convert_fusion.1
  538.0 5.6 multiply_convert_fusion.2
  548.0 5.4 multiply_convert_fusion.3
  557.9 4.6 multiply_convert_fusion.9
  562.7 20.5 %all-gather.3 = bf16[8,1,256]{2,1,0:T(2,128)(2,1)S(1)} all-gather(bf16[1,1,256]{2,1,0:T(2,128)(2,1)S(1)} %reshape.1422), channel_id=3, replica_groups=mesh['seq'=8,'tp'=4] {'seq'}, dimensions={0}, use_global_device_ids=true | all-gather | bytes 4608 | tf_op jit(solution)/shard_map/all_gather | solution.py:48
  592.4 4.1 fusion.97
  600.5 16.4 %all-gather.21.cloned.1.call-done = bf16[8,512,256]{2,1,0:T(8,128)(2,1)} async-done(((bf16[1,512,256]{2,1,0:T(8,128)(2,1)}), bf16[8,512,256]{2,1,0:T(8,128)(2,1)}) %all-gather.21.cloned.1.call-update) | async-done | bytes 2097168 | tf_op jit(solution)/shard_map/all_gather | solution.py:48
  617.0 8.4 while.30
  629.8 4.0 multiply_reduce_fusion.12
  662.7 32.1 %maximum_maximum_fusion = bf16[2048,768]{0,1:T(8,128)(2,1)S(1)} fusion(bf16[512,256]{0,1:T(8,128)(2,1)S(1)} %fusion.115, bf16[512,256]{0,1:T(8,128)(2,1)S(1)} %bitcast.550, bf16[512,256]{0,1:T(8,128)(2,1)S(1)} %bitcast.549, bf16[512,256]{0,1:T(8,128)(2,1)S(1)} %bitcast.548, bf16[512,256]{0,1:T(8,128)(2,1)S(1)} %fusion.116, ...), kind=kLoop, calls=%fused_computation.102 | loop fusion | flops 37748736 | bytes 6291456 | tf_op jit(solution)/shard_map/concatenate | solution.py:369
  696.5 5.1 fusion.216
  701.8 7.8 convolution_convert_fusion
  709.8 9.4 convolution_convert_fusion.1
  719.2 10.2 fusion.218
  729.7 10.1 fusion.219
  745.8 4.7 fusion.151
  750.6 17.1 %select_reduce_fusion = (f32[2]{0:T(128)S(1)}, f32[2]{0:T(128)S(1)}, f32[2]{0:T(128)S(1)}, f32[2]{0:T(128)S(1)}, f32[2]{0:T(128)S(1)}, /*index=5*/f32[2]{0:T(128...) fusion(pred[512,1024]{1,0:T(8,128)(4,1)} %get-tuple-element.518, ...), kind=kLoop, calls=%fused_computation.65 | loop fusion | flops 45088744 | bytes 22020240 | tf_op jit(solution)/shard_map/reduce_sum | solution.py:388
  772.4 11.3 select_reduce_fusion.18
  791.1 27.4 %reduce-scatter.19.cloned.1.call-done = bf16[512,1024]{1,0:T(8,128)(2,1)} async-done(((bf16[2048,1024]{1,0:T(8,128)(2,1)}), bf16[512,1024]{1,0:T(8,128)(2,1)}) %reduce-scatter.19.cloned.1.call-update) | async-done | bytes 1048592 | tf_op jit(solution)/shard_map/reduce_scatter | solution.py:378
  820.5 39.8 %all-reduce.5 = (f32[1024]{0:T(1024)}, f32[8,32]{1,0:T(8,128)}, f32[1024]{0:T(1024)}, f32[1024]{0:T(1024)}) all-reduce(f32[1024]{0:T(1024)S(1)} %get-tuple-element.327, f32[8,32]{1,0:T(8,128)S(1)} %constant_dynamic-update-slice_fusion.3, ...), channel_id=1, replica_groups=mesh['seq'=8,'tp'=4] {'seq','tp'}, use_global_device_ids=true, to_apply=%region_46.47 | all-reduce | flops 3328 | bytes 26624 | tf_op jit(solution)/shard_map/psum | solution.py:399
  860.4 6.1 reduce-scatter.15.cloned.1.call-done
  866.4 4.8 fusion.39
  871.3 87.3 %reduce-scatter.27.cloned.1.call-done = f32[128,1024]{1,0:T(8,128)} async-done(((f32[1024,1024]{1,0:T(8,128)}), f32[128,1024]{1,0:T(8,128)}) %reduce-scatter.27.cloned.1.call-update) | async-done | bytes 524304 | tf_op jit(solution)/shard_map/reduce_scatter | solution.py:408
  958.6 92.9 %reduce-scatter.29.cloned.1.call-done = f32[1024,128]{1,0:T(8,128)} async-done(((f32[1024,1024]{1,0:T(8,128)}), f32[1024,128]{1,0:T(8,128)}) %reduce-scatter.29.cloned.1.call-update) | async-done | bytes 524304 | tf_op jit(solution)/shard_map/reduce_scatter | solution.py:409
  1051.5 67.5 %reduce-scatter.23.cloned.1.call-done = f32[256,128]{1,0:T(8,128)} async-done(((f32[256,1024]{1,0:T(8,128)}), f32[256,128]{1,0:T(8,128)}) %reduce-scatter.23.cloned.1.call-update) | async-done | bytes 131088 | tf_op jit(solution)/shard_map/reduce_scatter | solution.py:405
  1119.0 65.1 %reduce-scatter.25.cloned.1.call-done = f32[64,256]{1,0:T(8,128)} async-done(((f32[512,256]{1,0:T(8,128)}), f32[64,256]{1,0:T(8,128)}) %reduce-scatter.25.cloned.1.call-update) | async-done | bytes 65552 | tf_op jit(solution)/shard_map/reduce_scatter | solution.py:406
  1184.1 64.7 %reduce-scatter.31.cloned.1.call-done = f32[64,256]{1,0:T(8,128)} async-done(((f32[512,256]{1,0:T(8,128)}), f32[64,256]{1,0:T(8,128)}) %reduce-scatter.31.cloned.1.call-update) | async-done | bytes 65552
  (643 shorter events, 222.5 us)
Async XLA Ops:
  7.2 320.8 %copy-start = (bf16[1024,1024]{1,0:T(8,128)(2,1)S(1)}, bf16[1024,1024]{1,0:T(8,128)(2,1)}, u32[]{:S(2)}) copy-start(bf16[1024,1024]{1,0:T(8,128)(2,1)} %param.33) | copy-start | bytes 6291460
  7.2 16.2 %copy-start.118 = (bf16[1024,256]{1,0:T(8,128)(2,1)S(1)}, bf16[1024,256]{1,0:T(8,128)(2,1)}, u32[]{:S(2)}) copy-start(bf16[1024,256]{1,0:T(8,128)(2,1)} %param.25) | copy-start | bytes 1572868
  7.2 46.7 %all-gather.11.cloned.1.call-start = ((), (), s32[]{:S(2)}) async-start(), calls=%async_computation.10 | async-start | bytes 5242880 | tf_op jit(solution)/shard_map/all_gather | solution.py:152
  9.5 18.7 %copy-start.168 = (f32[256]{0:T(256)S(1)}, f32[256]{0:T(256)}, u32[]{:S(2)}) copy-start(f32[256]{0:T(256)} %param.31) | copy-start | bytes 3076
  12.1 150.4 %all-gather.13.cloned.1.call-start = ((), (), s32[]{:S(2)}) async-start(), calls=%async_computation.11 | async-start | bytes 4718592 | tf_op jit(solution)/shard_map/all_gather | solution.py:28
  12.7 39.8 %collective-permute-start.1 = (s32[512]{0:T(512)}, s32[512]{0:T(512)}, u32[]{:S(2)}, u32[]{:S(2)}) collective-permute-start(s32[512]{0:T(512)} %get-tuple-element.447), channel_id=1, source_target_pairs={{0,4},{4,8},{8,12},{12,16},{16,20},{20,24},{24,28},{1,5},{5,9},{9,... | collective-permute-start | bytes 6152 | tf_op jit(solution)/shard_map/ppermute | solution.py:23
  20.4 62.7 %copy-start.46 = (bf16[512,256]{0,1:T(8,128)(2,1)}, bf16[512,256]{0,1:T(8,128)(2,1)S(1)}, u32[]{:S(2)}) copy-start(bf16[512,256]{0,1:T(8,128)(2,1)S(1)} %copy.416) | copy-start | bytes 786436
  28.8 147.3 %copy-start.126 = (f32[256]{0:T(256)}, f32[256]{0:T(256)S(1)}, u32[]{:S(2)}) copy-start(f32[256]{0:T(256)S(1)} %get-tuple-element.394) | copy-start | bytes 3076
  88.1 35.5 %copy-start.94 = (f32[2,128,512]{2,1,0:T(8,128)}, f32[2,128,512]{2,1,0:T(8,128)S(1)}, u32[]{:S(2)}) copy-start(f32[2,128,512]{2,1,0:T(8,128)S(1)} %fusion.135) | copy-start | bytes 1572868
  91.6 197.2 %reduce-scatter.13.cloned.1.call-start = ((), (), s32[]{:S(2)}) async-start(), calls=%async_computation.12 | async-start | bytes 10485760 | tf_op jit(solution)/shard_map/reduce_scatter | solution.py:244
  151.0 31.3 %collective-permute-start = (bf16[512,256]{0,1:T(8,128)(2,1)}, bf16[512,256]{0,1:T(8,128)(2,1)}, u32[]{:S(2)}, u32[]{:S(2)}) collective-permute-start(bf16[512,256]{0,1:T(8,128)(2,1)} %get-tuple-element.415), channel_id=1, source_target_pairs={{0,4},{4,8},{8,12},{12,16},{16,20},{20,24},{24,28},{1,5},{5,9},{9,... | collective-permute-start | bytes 786440 | tf_op jit(solution)/shard_map/ppermute | solution.py:23
  153.6 29.4 %collective-permute-start.2 = (bf16[512,256]{0,1:T(8,128)(2,1)}, bf16[512,256]{0,1:T(8,128)(2,1)}, u32[]{:S(2)}, u32[]{:S(2)}) collective-permute-start(bf16[512,256]{0,1:T(8,128)(2,1)} %copy-done.101), channel_id=1, source_target_pairs={{0,4},{4,8},{8,12},{12,16},{16,20},{20,24},{24,28},{1,5},{5,9},{9,... | collective-permute-start | bytes 786440 | tf_op jit(solution)/shard_map/ppermute | solution.py:23
  184.4 17.8 %copy-start.38 = (bf16[1536,256]{0,1:T(8,128)(2,1)}, bf16[1536,256]{0,1:T(8,128)(2,1)S(1)}, u32[]{:S(2)}) copy-start(bf16[1536,256]{0,1:T(8,128)(2,1)S(1)} %get-tuple-element.440) | copy-start | bytes 2359300
  186.4 15.8 %copy-start.2 = (f32[2,512,1536]{2,1,0:T(8,128)}, f32[2,512,1536]{2,1,0:T(8,128)S(1)}, u32[]{:S(2)}) copy-start(f32[2,512,1536]{2,1,0:T(8,128)S(1)} %get-tuple-element.545) | copy-start | bytes 18874372
  212.8 76.0 %copy-start.15 = (bf16[512,1024]{1,0:T(8,128)(2,1)S(1)}, bf16[512,1024]{1,0:T(8,128)(2,1)}, u32[]{:S(2)}) copy-start(bf16[512,1024]{1,0:T(8,128)(2,1)} %param.20) | copy-start | bytes 3145732
  212.8 79.3 %copy-start.128 = (f32[1024]{0:T(1024)S(1)}, f32[1024]{0:T(1024)}, u32[]{:S(2)}) copy-start(f32[1024]{0:T(1024)} %param.32) | copy-start | bytes 12292
  212.8 115.2 %all-gather.15.cloned.1.call-start = ((), (), s32[]{:S(2)}) async-start(), calls=%async_computation.13 | async-start | bytes 5242880 | tf_op jit(solution)/shard_map/all_gather | solution.py:253
  290.8 167.4 %copy-start.130 = (f32[512]{0:T(512)}, f32[512]{0:T(512)S(1)}, u32[]{:S(2)}) copy-start(f32[512]{0:T(512)S(1)} %add_rsqrt_fusion) | copy-start | bytes 6148
  293.3 70.6 %all-gather.17.cloned.1.call-start = ((), (), s32[]{:S(2)}) async-start(), calls=%async_computation.15 | async-start | bytes 5242880 | tf_op jit(solution)/shard_map/all_gather | solution.py:267
  293.9 161.3 %reduce-scatter.17.cloned.1.call-start = ((), (), s32[]{:S(2)}) async-start(), calls=%async_computation.16 | async-start | bytes 10485760 | tf_op jit(solution)/shard_map/reduce_scatter | solution.py:273
  383.3 71.9 %copy-start.8 = (f32[512,1024]{1,0:T(8,128)S(1)}, f32[512,1024]{1,0:T(8,128)}, u32[]{:S(2)}) copy-start(f32[512,1024]{1,0:T(8,128)} %copy-done.7) | copy-start | bytes 6291460
  383.3 74.8 %copy-start.21 = (bf16[512,1024]{1,0:T(8,128)(2,1)S(1)}, bf16[512,1024]{1,0:T(8,128)(2,1)}, u32[]{:S(2)}) copy-start(bf16[512,1024]{1,0:T(8,128)(2,1)} %param.35) | copy-start | bytes 3145732
  383.3 111.1 %all-gather.19.cloned.1.call-start = ((), (), s32[]{:S(2)}) async-start(), calls=%async_computation.17 | async-start | bytes 5242880 | tf_op jit(solution)/shard_map/all_gather | solution.py:279
  459.8 157.2 %all-gather.21.cloned.1.call-start = ((), (), s32[]{:S(2)}) async-start(), calls=%async_computation.18 | async-start | bytes 2359296 | tf_op jit(solution)/shard_map/all_gather | solution.py:48
  502.5 24.5 %copy-start.60 = (f32[1536,2,128]{0,2,1:T(8,128)}, f32[1536,2,128]{0,2,1:T(8,128)S(1)}, u32[]{:S(2)}) copy-start(f32[1536,2,128]{0,2,1:T(8,128)S(1)} %convolution_bitcast_fusion.1) | copy-start | bytes 4718596
  555.7 33.6 %copy-start.32 = (bf16[1536,256]{0,1:T(8,128)(2,1)S(1)}, bf16[1536,256]{0,1:T(8,128)(2,1)}, u32[]{:S(2)}) copy-start(bf16[1536,256]{0,1:T(8,128)(2,1)} %copy-done.31) | copy-start | bytes 2359300
  556.9 35.5 %copy-start.58 = (f32[512,2,128]{0,2,1:T(8,128)}, f32[512,2,128]{0,2,1:T(8,128)S(1)}, u32[]{:S(2)}) copy-start(f32[512,2,128]{0,2,1:T(8,128)S(1)} %slice_add_fusion.5) | copy-start | bytes 1572868
  562.6 226.8 %reduce-scatter.21.cloned.1.call-start = ((), (), s32[]{:S(2)}) async-start(), calls=%async_computation.20 | async-start | bytes 3538944 | tf_op jit(solution)/shard_map/reduce_scatter | solution.py:404
  586.7 73.7 %collective-permute-start.3 = (bf16[512,256]{0,1:T(8,128)(2,1)}, bf16[512,256]{0,1:T(8,128)(2,1)}, u32[]{:S(2)}, u32[]{:S(2)}) collective-permute-start(bf16[512,256]{0,1:T(8,128)(2,1)} %bitcast.105), channel_id=1, source_target_pairs={{4,0},{8,4},{12,8},{16,12},{20,16},{24,20},{28,24},{5,1},{9,5},{13... | collective-permute-start | bytes 786440 | tf_op jit(solution)/shard_map/ppermute | solution.py:23
  588.0 73.5 %collective-permute-start.4 = (bf16[512,256]{0,1:T(8,128)(2,1)}, bf16[512,256]{0,1:T(8,128)(2,1)}, u32[]{:S(2)}, u32[]{:S(2)}) collective-permute-start(bf16[512,256]{0,1:T(8,128)(2,1)} %bitcast.115), channel_id=1, source_target_pairs={{4,0},{8,4},{12,8},{16,12},{20,16},{24,20},{28,24},{5,1},{9,5},{13... | collective-permute-start | bytes 786440 | tf_op jit(solution)/shard_map/ppermute | solution.py:23
  662.7 33.7 %copy-start.170 = (bf16[2048,1024]{1,0:T(8,128)(2,1)S(1)}, bf16[2048,1024]{1,0:T(8,128)(2,1)}, u32[]{:S(2)}) copy-start(bf16[2048,1024]{1,0:T(8,128)(2,1)} %all-gather.11.cloned.1.call-done) | copy-start | bytes 12582916
  701.6 116.9 %reduce-scatter.19.cloned.1.call-start = ((), (), s32[]{:S(2)}) async-start(), calls=%async_computation.19 | async-start | bytes 5242880 | tf_op jit(solution)/shard_map/reduce_scatter | solution.py:378
  709.7 156.7 %reduce-scatter.15.cloned.1.call-start = ((), (), s32[]{:S(2)}) async-start(), calls=%async_computation.14 | async-start | bytes 5242880 | tf_op jit(solution)/shard_map/reduce_scatter | solution.py:260
  719.2 239.4 %reduce-scatter.27.cloned.1.call-start = ((), (), s32[]{:S(2)}) async-start(), calls=%async_computation.23 | async-start | bytes 4718592 | tf_op jit(solution)/shard_map/reduce_scatter | solution.py:408
  729.4 322.0 %reduce-scatter.29.cloned.1.call-start = ((), (), s32[]{:S(2)}) async-start(), calls=%async_computation.24 | async-start | bytes 4718592 | tf_op jit(solution)/shard_map/reduce_scatter | solution.py:409
  739.8 379.2 %reduce-scatter.23.cloned.1.call-start = ((), (), s32[]{:S(2)}) async-start(), calls=%async_computation.21 | async-start | bytes 1179648 | tf_op jit(solution)/shard_map/reduce_scatter | solution.py:405
  750.5 433.6 %reduce-scatter.25.cloned.1.call-start = ((), (), s32[]{:S(2)}) async-start(), calls=%async_computation.22 | async-start | bytes 589824 | tf_op jit(solution)/shard_map/reduce_scatter | solution.py:406
  750.6 17.1 %copy-start.74 = (bf16[512,256]{0,1:T(8,128)(2,1)S(1)}, bf16[512,256]{0,1:T(8,128)(2,1)}, u32[]{:S(2)}) copy-start(bf16[512,256]{0,1:T(8,128)(2,1)} %copy-done.72) | copy-start | bytes 786436
  750.6 17.5 %copy-start.104 = (bf16[512,256]{0,1:T(8,128)(2,1)S(1)}, bf16[512,256]{0,1:T(8,128)(2,1)}, u32[]{:S(2)}) copy-start(bf16[512,256]{0,1:T(8,128)(2,1)} %get-tuple-element.411) | copy-start | bytes 786436
  772.2 476.6 %reduce-scatter.31.cloned.1.call-start = ((), (), s32[]{:S(2)}) async-start(), calls=%async_computation.25 | async-start | bytes 589824
  772.3 46.1 %copy-start.134 = (f32[1024]{0:T(1024)S(1)}, f32[1024]{0:T(1024)}, u32[]{:S(2)}) copy-start(f32[1024]{0:T(1024)} %param.24) | copy-start | bytes 12292
  772.4 46.1 %copy-start.137 = (f32[512]{0:T(512)S(1)}, f32[512]{0:T(512)}, u32[]{:S(2)}) copy-start(f32[512]{0:T(512)} %copy-done.136) | copy-start | bytes 6148
  783.7 34.8 %copy-start.16 = (bf16[512,1024]{1,0:T(8,128)(2,1)S(1)}, bf16[512,1024]{1,0:T(8,128)(2,1)}, u32[]{:S(2)}) copy-start(bf16[512,1024]{1,0:T(8,128)(2,1)} %param.20) | copy-start | bytes 3145732
  783.7 36.8 %copy-start.140 = (f32[1024]{0:T(1024)S(1)}, f32[1024]{0:T(1024)}, u32[]{:S(2)}) copy-start(f32[1024]{0:T(1024)} %get-tuple-element.293) | copy-start | bytes 12292
  783.7 82.7 %copy-start.129 = (f32[1024]{0:T(1024)S(1)}, f32[1024]{0:T(1024)}, u32[]{:S(2)}) copy-start(f32[1024]{0:T(1024)} %param.32) | copy-start | bytes 12292
  783.7 82.7 %copy-start.131 = (f32[512]{0:T(512)S(1)}, f32[512]{0:T(512)}, u32[]{:S(2)}) copy-start(f32[512]{0:T(512)} %copy-done.130) | copy-start | bytes 6148
  783.7 82.7 %copy-start.139 = (f32[512]{0:T(512)S(1)}, f32[512]{0:T(512)}, u32[]{:S(2)}) copy-start(f32[512]{0:T(512)} %copy-done.138) | copy-start | bytes 6148
  860.4 388.4 %copy-start.1 = (bf16[1024,1024]{1,0:T(8,128)(2,1)S(1)}, bf16[1024,1024]{1,0:T(8,128)(2,1)}, u32[]{:S(2)}) copy-start(bf16[1024,1024]{1,0:T(8,128)(2,1)} %param.33) | copy-start | bytes 6291460
  (154 other events, 579.8 us)
Sparse Core Ops, SparseCore 0:
  12.2 37.1 all-gather.10
  91.7 70.6 all-gather.12
  212.9 75.8 reduce-scatter.12
  293.4 34.4 all-gather.14
  329.5 34.4 all-gather.16
  383.4 71.7 reduce-scatter.16
  459.9 34.4 all-gather.18
  562.7 54.1 all-gather.20
  701.7 70.6 reduce-scatter.20
  774.8 43.6 reduce-scatter.18
  821.2 45.2 reduce-scatter.14
  870.5 88.0 reduce-scatter.26
  963.3 88.1 reduce-scatter.28
  1055.3 63.5 reduce-scatter.22
  1123.1 60.9 reduce-scatter.24
  1187.9 60.9 reduce-scatter.30
where the time goes:
time: 1270 us; the launch traced here: 1260 us
  waiting for transfers between devices  659 us (52%)
  other arithmetic  222 us (17%)
  matrix products  197 us (16%)
  blocking collectives  78.6 us (6%)
  local copies, waits for them, and re-layouts  67.7 us (5%)
  between operations  16.9 us (1%)
  starting transfers between devices  14.1 us (1%)
    reduce_scatter x1, waiting for transfers between devices, local(): lax.psum_scatter(grad_return_sum, 'seq', scatter_dimension=1, tiled=True)  92.9 us
    reduce_scatter x1, waiting for transfers between devices, local(): lax.psum_scatter(grad_hidden_w, 'seq', scatter_dimension=0, tiled=True)  87.3 us
    reduce_scatter x1, waiting for transfers between devices, local(): lax.psum_scatter(jnp.dot(output_low, w_output, preferred_element_type=jnp...  75.9 us
    reduce_scatter x1, waiting for transfers between devices, local(): lax.psum_scatter(contract(mlp_grad_pre, w_hidden, 1, 1), 'tp', scatter_di...  71.8 us
    reduce_scatter x1, waiting for transfers between devices, local(): lax.psum_scatter(grad_w_sum, 'seq', scatter_dimension=1, tiled=True)  67.5 us
    unnamed x17, waiting for transfers between devices  65.5 us
    reduce_scatter x1, waiting for transfers between devices, local(): lax.psum_scatter(queries_flat, 'seq', scatter_dimension=0, tiled=True)  65.1 us
    dot_general x8, matrix products, contract(): lax.dot_general(left, right, (((left_dim,), (right_dim,)), ((), ())), pre...  58.8 us
  transfers between devices with their start and end apart: 21, of which 14 were waited for; matrix products, arithmetic and copies ran while one was open for 22% of the time, Pallas kernels for 0%

commit v1 on v0

v1 whole, which is shorter than its diff:
```python
import functools
import math

import jax
import jax.numpy as jnp
import numpy as np
from jax import lax
from jax.experimental import pallas as pl
from jax.experimental.pallas import tpu as pltpu
from jax.sharding import PartitionSpec as P

D = 1024
H = 8
NS = 512
BLOCK = 512
BUCKETS = 32
FAR = 128
TILE = 128
SPAN = BLOCK + TILE
HEAD = 128

eps = 1e-06
negative_fill = -1e30
LOG2E = math.log2(math.e)
f32 = jnp.float32
bf16 = jnp.bfloat16
VMEM_LIMIT = 56 * 1024 * 1024


def nn(a, b):
    return lax.dot_general(a, b, (((1,), (0,)), ((), ())), preferred_element_type=f32)


def nt(a, b):
    return lax.dot_general(a, b, (((1,), (1,)), ((), ())), preferred_element_type=f32)


def tn(a, b):
    return lax.dot_general(a, b, (((0,), (0,)), ((), ())), preferred_element_type=f32)


def call(kernel, grid, prefetch, ins, outs, aliases=(), scratch=(), flops=0, nbytes=0, exps=0):
    any_spec = pl.BlockSpec(memory_space=pl.ANY)
    arrays = [array for array, _ in ins] + [array for array, _ in aliases]
    specs = [spec for _, spec in ins] + [any_spec for _ in aliases]
    first = len(prefetch) + len(ins)
    alias_map = {first + n: out for n, (_, out) in enumerate(aliases)}
    n_pre, n_in, n_alias = len(prefetch), len(ins), len(aliases)

    def body(*refs):
        kept = refs[: n_pre + n_in] + refs[n_pre + n_in + n_alias :]
        kernel(*kept)

    return pl.pallas_call(
        body,
        out_shape=[jax.ShapeDtypeStruct(shape, dtype) for shape, dtype, _ in outs],
        grid_spec=pltpu.PrefetchScalarGridSpec(
            num_scalar_prefetch=n_pre,
            grid=grid,
            in_specs=specs,
            out_specs=[spec for _, _, spec in outs],
            scratch_shapes=list(scratch),
        ),
        input_output_aliases=alias_map,
        compiler_params=pltpu.CompilerParams(
            dimension_semantics=("arbitrary",) * len(grid), vmem_limit_bytes=VMEM_LIMIT
        ),
        cost_estimate=pl.CostEstimate(
            flops=int(flops), bytes_accessed=int(nbytes), transcendentals=int(exps)
        ),
    )(*prefetch, *arrays)


def lanes(*columns):
    rows = columns[0].shape[0]
    lane = lax.broadcasted_iota(jnp.int32, (rows, 128), 1)
    packed = jnp.broadcast_to(columns[0], (rows, 128))
    for n, column in enumerate(columns[1:], 1):
        packed = jnp.where(lane == n, column, packed)
    return packed


def head_of(h):
    return slice(h * HEAD, (h + 1) * HEAD)


def bias_kernel(base_ref, out_ref):
    for h in range(out_ref.shape[0]):
        row = jnp.broadcast_to(base_ref[h : h + 1, :], (TILE, SPAN))
        out_ref[h] = pltpu.roll(row, 0, 1, stride=1, stride_axis=0)


def bias_sum_kernel(grad_ref, out_ref):
    rows = lax.broadcasted_iota(jnp.int32, (TILE, SPAN), 0)
    for h in range(grad_ref.shape[0]):
        value = grad_ref[h]
        step = 1
        while step < TILE:
            moved = pltpu.roll(value, SPAN - step, 1)
            value = jnp.where((rows & step) != 0, moved, value)
            step *= 2
        out_ref[h : h + 1, :] = jnp.sum(value, axis=0, keepdims=True)


def front_kernel(scale, heads, tok, gain, w, sq, normed_out, qkv_out, u_out, lse_out):
    width = heads * HEAD
    rows = 256
    for i in range(BLOCK // rows):
        part = slice(i * rows, (i + 1) * rows)
        x = tok[part, :].astype(f32)
        r = lax.rsqrt(jnp.mean(x * x, axis=-1, keepdims=True) + eps)
        n = (x * r * gain[...]).astype(bf16)
        normed_out[part, :] = n
        qkv_out[part, :] = nn(n, w[...]).astype(bf16)
    for i in range(BLOCK // rows):
        part = slice(i * rows, (i + 1) * rows)
        stats = []
        for h in range(heads):
            k = qkv_out[:, width + h * HEAD : width + (h + 1) * HEAD]
            v = qkv_out[:, 2 * width + h * HEAD : 2 * width + (h + 1) * HEAD]
            s = nt(sq[part, head_of(h)], k) * (scale * LOG2E)
            m = jnp.max(s, axis=1, keepdims=True)
            p = jnp.exp2(s - m)
            l = jnp.sum(p, axis=1, keepdims=True)
            u_out[0, part, head_of(h)] = nn(p.astype(bf16), v) / l
            stats.append(m + jnp.log(l) * LOG2E)
        lse_out[0, part, :] = lanes(*stats)


def window_scores(scale, h, i, q, kp, kc, qid, idp, idc, bias):
    r0 = i * TILE
    cut = BLOCK - r0
    qc = qid[r0 : r0 + TILE, :]
    s1 = nt(q, kp[r0:, head_of(h)]) * (scale * LOG2E) + bias[h, :, :cut]
    s2 = nt(q, kc[: r0 + TILE, head_of(h)]) * (scale * LOG2E) + bias[h, :, cut:]
    s1 = jnp.where(qc == idp[0, :, r0:], s1, negative_fill)
    s2 = jnp.where(qc == idc[0, :, : r0 + TILE], s2, negative_fill)
    return s1, s2


def window_kernel(scale, heads, t, q, kc, vc, hk, hv, qid, idp, idc, bias, acc, ml, kp, vp):
    j = pl.program_id(0)

    @pl.when(j == 0)
    def _():
        kp[...] = hk[...]
        vp[...] = hv[...]

    for i in range(BLOCK // TILE):
        r0 = i * TILE
        part = slice(r0, r0 + TILE)
        peaks, sums = [], []
        for h in range(heads):
            qt = q[part, head_of(h)]
            s1, s2 = window_scores(scale, h, i, qt, kp, kc, qid, idp, idc, bias)
            m = jnp.maximum(
                jnp.max(s1, axis=1, keepdims=True), jnp.max(s2, axis=1, keepdims=True)
            )
            p1 = jnp.exp2(s1 - m)
            p2 = jnp.exp2(s2 - m)
            peaks.append(m)
            sums.append(jnp.sum(p1, axis=1, keepdims=True) + jnp.sum(p2, axis=1, keepdims=True))
            acc[0, part, head_of(h)] = nn(p1.astype(bf16), vp[r0:, head_of(h)]) + nn(
                p2.astype(bf16), vc[: r0 + TILE, head_of(h)]
            )
        ml[0, part, :] = lanes(*peaks, *sums)
    kp[...] = kc[...]
    vp[...] = vc[...]


def state_kernel(
    scale, heads, t, q, entry, before, carry_row, keep_row, gates, u, acc, ml, w,
    mixed_out, stats_out, used_out, next_out, part_out,
):
    used = carry_row[0] * entry[...] + keep_row[0] * before[0]
    next_out[0] = gates[...] * used + u[0]
    used_out[0] = used.astype(bf16)
    rows = 256
    for i in range(BLOCK // rows):
        part = slice(i * rows, (i + 1) * rows)
        stats = []
        for h in range(heads):
            state = used_out[0, :, head_of(h)]
            m = ml[0, part, h : h + 1]
            l = ml[0, part, heads + h : heads + h + 1]
            s = nt(q[part, head_of(h)], state) * (scale * LOG2E)
            top = jnp.maximum(m, jnp.max(s, axis=1, keepdims=True))
            p = jnp.exp2(s - top)
            shrink = jnp.exp2(m - top)
            total = l * shrink + jnp.sum(p, axis=1, keepdims=True)
            value = (acc[0, part, head_of(h)] * shrink + nn(p.astype(bf16), state)) / total
            mixed_out[0, part, head_of(h)] = value.astype(bf16)
            stats.append(top + jnp.log(total) * LOG2E)
        stats_out[0, part, :] = lanes(*stats)
        part_out[part, :] = nn(mixed_out[0, part, :], w[...]).astype(bf16)


def mlp_kernel(nm, gact, w, hidden_out, gpre_out, part_out):
    cols = 256
    total = None
    for c in range(w.shape[1] // cols):
        cut = slice(c * cols, (c + 1) * cols)
        pre = nn(nm[...], w[:, cut])
        cumulative = 0.5 * (1.0 + lax.erf(pre * (1.0 / math.sqrt(2.0))))
        density = jnp.exp2(pre * pre * (-0.5 * LOG2E)) * (1.0 / math.sqrt(2.0 * math.pi))
        hidden_out[:, cut] = (pre * cumulative).astype(bf16)
        gpre = (gact[:, cut].astype(f32) * (cumulative + pre * density)).astype(bf16)
        gpre_out[:, cut] = gpre
        piece = nt(gpre, w[:, cut])
        total = piece if total is None else total + piece
    part_out[...] = total.astype(bf16)


def state_back_kernel(
    scale, heads, ga, w, q, mixed, used, stats, gm_out, stats_out, dq_out, direct_out
):
    step = pl.program_id(0)
    gm_all = nt(ga[...], w[...]).astype(bf16)
    gm_out[0] = gm_all
    logs, deltas = [], []
    for h in range(heads):
        gm = gm_all[:, head_of(h)]
        qt = q[:, head_of(h)]
        state = used[0, :, head_of(h)]
        delta = jnp.sum(
            gm.astype(f32) * mixed[0, :, head_of(h)].astype(f32), axis=1, keepdims=True
        )
        lse = stats[0, :, h : h + 1]
        p = jnp.exp2(nt(qt, state) * (scale * LOG2E) - lse)
        ds = (p * (nt(gm, state) - delta)).astype(bf16)
        dq_out[0, :, head_of(h)] = nn(ds, state) * scale
        du = tn(ds, qt) * scale + tn(p.astype(bf16), gm)
        logs.append(lse)
        deltas.append(delta)

        @pl.when(step == 0)
        def _():
            direct_out[0, :, head_of(h)] = du

        @pl.when(step != 0)
        def _():
            direct_out[0, :, head_of(h)] += du

    stats_out[0] = lanes(*logs, *deltas)


def window_back_kernel(
    scale, heads, t, q, kc, vc, kb, vb, hk, hv, qid, idp, idc, bias, gm, stats, dqs,
    dq_out, dk_out, dv_out, hk_out, hv_out, grad_bias, kp, vp, dkp, dvp, dkc, dvc,
):
    step = pl.program_id(0)
    last = pl.num_programs(0) - 1

    @pl.when(step == last)
    def _():
        kp[...] = hk[...]
        vp[...] = hv[...]

    @pl.when(step != last)
    def _():
        kp[...] = kb[...]
        vp[...] = vb[...]

    @pl.when(step == 0)
    def _():
        dkp[...] = jnp.zeros_like(dkp)
        dvp[...] = jnp.zeros_like(dvp)
        grad_bias[...] = jnp.zeros_like(grad_bias)

    dkc[...] = dkp[...]
    dvc[...] = dvp[...]
    dkp[...] = jnp.zeros_like(dkp)
    dvp[...] = jnp.zeros_like(dvp)
    for i in range(BLOCK // TILE):
        r0 = i * TILE
        cut = BLOCK - r0
        r1 = r0 + TILE
        part = slice(r0, r1)
        for h in range(heads):
            hs = head_of(h)
            qt = q[part, hs]
            g = gm[0, part, hs]
            lse = stats[0, part, h : h + 1]
            delta = stats[0, part, heads + h : heads + h + 1]
            s1, s2 = window_scores(scale, h, i, qt, kp, kc, qid, idp, idc, bias)
            p1 = jnp.exp2(s1 - lse)
            p2 = jnp.exp2(s2 - lse)
            ds1 = p1 * (nt(g, vp[r0:, hs]) - delta)
            ds2 = p2 * (nt(g, vc[:r1, hs]) - delta)
            grad_bias[h, :, :cut] += ds1
            grad_bias[h, :, cut:] += ds2
            ds1 = ds1.astype(bf16)
            ds2 = ds2.astype(bf16)
            dq = (nn(ds1, kp[r0:, hs]) + nn(ds2, kc[:r1, hs])) * scale + dqs[0, part, hs]
            dq_out[part, hs] = dq.astype(bf16)
            dkp[r0:, hs] += tn(ds1, qt) * scale
            dkc[:r1, hs] += tn(ds2, qt) * scale
            dvp[r0:, hs] += tn(p1.astype(bf16), g)
            dvc[:r1, hs] += tn(p2.astype(bf16), g)
    dk_out[0] = dkc[...]
    dv_out[0] = dvc[...]

    @pl.when(step == last)
    def _():
        hk_out[...] = dkp[...].astype(bf16)
        hv_out[...] = dvp[...].astype(bf16)


def update_back_kernel(
    scale, heads, t, carried0, direct, entry, before, carry_row, keep_row, gates, k, v, sq,
    lse_u, u, dq, dk, dv, hk, hv, w, dkv_out, part_out, dsq_out, gate_out, carried,
):
    step = pl.program_id(0)
    width = heads * HEAD

    @pl.when(step == 0)
    def _():
        carried[...] = carried0[...]
        dsq_out[...] = jnp.zeros_like(dsq_out)
        gate_out[...] = jnp.zeros_like(gate_out)

    used = carry_row[0] * entry[...] + keep_row[0] * before[0]
    now = carried[...]
    gate_out[...] += jnp.sum(now * used, axis=0, keepdims=True)
    gu_all = now.astype(bf16)
    carried[...] = keep_row[0] * (direct[0] + gates[...] * now)
    for h in range(heads):
        hs = head_of(h)
        gu = gu_all[:, hs]
        sqh = sq[:, hs]
        kh = k[:, hs]
        delta = jnp.sum(gu.astype(f32) * u[0, :, hs], axis=1, keepdims=True)
        p = jnp.exp2(nt(sqh, kh) * (scale * LOG2E) - lse_u[0, :, h : h + 1])
        ds = (p * (nt(gu, v[:, hs]) - delta)).astype(bf16)
        dsq_out[:, hs] += nn(ds, kh) * scale
        more = jnp.where(step == 0, 1.0, 0.0)
        dkh = dk[0, :, hs] + tn(ds, sqh) * scale + more * hk[:, hs].astype(f32)
        dvh = dv[0, :, hs] + tn(p.astype(bf16), gu) + more * hv[:, hs].astype(f32)
        dkv_out[:, hs] = dkh.astype(bf16)
        dkv_out[:, width + h * HEAD : width + (h + 1) * HEAD] = dvh.astype(bf16)
    part = nt(dq[...], w[:, :width]) + nt(dkv_out[...], w[:, width:])
    part_out[...] = part.astype(bf16)


def bucket_of(distance):
    half = BUCKETS // 2
    limits = [math.ceil(half * (FAR / half) ** (level / half)) for level in range(1, half)]
    clipped = np.maximum(distance, 0)
    extra = sum((clipped >= limit).astype(np.int32) for limit in limits)
    return np.where(clipped < half, clipped, half + extra)


def local(
    tokens,
    doc_flags,
    reset_flags,
    state_init,
    gain_attn,
    w_query,
    w_key,
    w_value,
    w_output,
    bias_table,
    state_queries,
    gate_logits,
    gain_mlp,
    w_hidden,
    w_return,
    cotangent,
):
    heads = bias_table.shape[0]
    lw = w_query.shape[1]
    width = tokens.shape[1]
    nb = reset_flags.shape[0]
    ff = w_hidden.shape[1]
    scale = 1.0 / math.sqrt(HEAD)
    groups = lax.axis_size("seq")
    s_index = lax.axis_index("seq")
    t_index = lax.axis_index("tp")
    t_pre = t_index.astype(jnp.int32)[None]
    rows_all = nb * BLOCK

    def core(value):
        return lax.ppermute(value, "tp", [(i, i ^ 1) for i in range(nb)])

    def cross(value):
        return lax.ppermute(value, "tp", [(i, i ^ 2) for i in range(nb)])

    def along(value, step):
        pairs = [(i, i + step) for i in range(groups) if 0 <= i + step < groups]
        return lax.ppermute(value, "seq", pairs)

    full = lambda *shape: pl.BlockSpec(shape, lambda *_: (0,) * len(shape))

    tok2 = cross(tokens)
    cot2 = cross(cotangent)
    toks = [tokens, core(tokens), tok2, core(tok2)]
    cots = [cotangent, core(cotangent), cot2, core(cot2)]

    every = reset_flags.reshape(1, nb)
    step = 1
    while step < groups:
        every = jnp.concatenate(
            [every, lax.ppermute(every, "seq", [(i, i ^ step) for i in range(groups)])]
        )
        step *= 2
    group_of = jnp.arange(groups, dtype=jnp.int32) ^ s_index
    group_keep = jnp.prod((1 - every).astype(f32), axis=1)

    def keep_between(low, high):
        inside = (group_of >= low) & (group_of <= high)
        return jnp.prod(jnp.where(inside, group_keep, 1.0))

    gates = jax.nn.sigmoid(gate_logits)
    keeps = (1 - reset_flags).astype(f32)
    gate_row = gates[None, :]

    def gate_power(count):
        result, base = None, gates
        while count:
            if count & 1:
                result = base if result is None else result * base
            base = base * base
            count >>= 1
        return jnp.ones_like(gates) if result is None else result

    flag_prev = along(doc_flags[rows_all - BLOCK :], 1)
    ids = jnp.cumsum(jnp.concatenate([flag_prev, doc_flags]))
    ids = jnp.where((jnp.arange(rows_all + BLOCK) < BLOCK) & (s_index == 0), -1, ids)
    id_rows = ids.reshape(nb + 1, 1, BLOCK)
    id_cols = ids[BLOCK:].reshape(rows_all, 1)

    apart = BLOCK - np.arange(SPAN)
    shown = (apart >= 0) & (apart < BLOCK)
    onehot = (bucket_of(apart)[:, None] == np.arange(BUCKETS)[None, :]) & shown[:, None]
    onehot = jnp.asarray(onehot.astype(np.float32))
    base = jnp.dot(bias_table * LOG2E, onehot.T, precision=lax.Precision.HIGHEST)
    base = jnp.where(jnp.asarray(shown)[None, :], base, negative_fill)
    (bias,) = call(
        bias_kernel,
        (1,),
        (),
        [(base, full(heads, SPAN))],
        [((heads, TILE, SPAN), f32, full(heads, TILE, SPAN))],
    )

    w_joined = jnp.concatenate([w_query, w_key, w_value], axis=1)
    stacked = None
    for r in range(nb):
        aliases = [] if stacked is None else [(array, n) for n, array in enumerate(stacked)]
        stacked = call(
            functools.partial(front_kernel, scale, heads),
            (1,),
            (),
            [
                (toks[r], full(BLOCK, width)),
                (gain_attn[None, :], full(1, width)),
                (w_joined, full(width, 3 * lw)),
                (state_queries, full(NS, lw)),
            ],
            [
                ((rows_all, width), bf16, pl.BlockSpec((BLOCK, width), lambda g, r=r: (r, 0))),
                ((rows_all, 3 * lw), bf16, pl.BlockSpec((BLOCK, 3 * lw), lambda g, r=r: (r, 0))),
                ((nb, NS, lw), f32, pl.BlockSpec((1, NS, lw), lambda g, r=r: (r, 0, 0))),
                ((nb, NS, 128), f32, pl.BlockSpec((1, NS, 128), lambda g, r=r: (r, 0, 0))),
            ],
            aliases,
            flops=2 * BLOCK * width * 3 * lw + 4 * NS * BLOCK * lw,
            nbytes=6 * BLOCK * width * 2,
            exps=heads * NS * BLOCK,
        )
    normed_all, qkv, updates, lse_u = stacked

    def in_order(array, j):
        return lax.dynamic_index_in_dim(array, t_index ^ j, 0, False)

    factors = [gates * keeps[j] for j in range(nb)]
    before = [jnp.zeros((NS, lw), f32)]
    factor_before = [jnp.ones_like(gates)]
    for j in range(nb):
        before.append(factors[j] * before[j] + in_order(updates, j))
        factor_before.append(factor_before[j] * factors[j])
    total = before.pop()
    factor_total = factor_before.pop()
    before = jnp.stack(before)
    entry = jnp.zeros((NS, lw), f32)
    step = 1
    while step < groups:
        sent = (factor_total * entry + total).astype(bf16)
        got = along(sent, step).astype(f32)
        kept = keep_between(s_index - step + 1, s_index - 1)
        entry = (gate_power(nb * (step - 1)) * kept) * got + entry
        step *= 2
    power, bit = jnp.ones_like(gates), 1
    while bit < groups:
        power = power * jnp.where((s_index & bit) != 0, gate_power(nb * bit), 1.0)
        bit *= 2
    prefix_factor = power * keep_between(0, s_index - 1)
    entry = prefix_factor * state_init + entry
    carry_rows = (jnp.stack(factor_before) * keeps[:, None])[:, None, :]
    keep_rows = jnp.broadcast_to(keeps[:, None, None], (nb, 1, lw))

    place = (t_index ^ (nb - 1)) * BLOCK
    edge = along(lax.dynamic_slice(qkv, (place, lw), (BLOCK, 2 * lw)), 1)
    at = lambda col: pl.BlockSpec((BLOCK, lw), lambda j, t: (j ^ t[0], col))
    pair_flops = 2 * BLOCK * SPAN * lw
    acc, ml = call(
        functools.partial(window_kernel, scale, heads),
        (nb,),
        (t_pre,),
        [
            (qkv, at(0)),
            (qkv, at(1)),
            (qkv, at(2)),
            (edge, pl.BlockSpec((BLOCK, lw), lambda j, t: (0, 0))),
            (edge, pl.BlockSpec((BLOCK, lw), lambda j, t: (0, 1))),
            (id_cols, pl.BlockSpec((BLOCK, 1), lambda j, t: (j, 0))),
            (id_rows, pl.BlockSpec((1, 1, BLOCK), lambda j, t: (j, 0, 0))),
            (id_rows, pl.BlockSpec((1, 1, BLOCK), lambda j, t: (j + 1, 0, 0))),
            (bias, full(heads, TILE, SPAN)),
        ],
        [
            ((nb, BLOCK, lw), f32, pl.BlockSpec((1, BLOCK, lw), lambda j, t: (j, 0, 0))),
            ((nb, BLOCK, 128), f32, pl.BlockSpec((1, BLOCK, 128), lambda j, t: (j, 0, 0))),
        ],
        scratch=[pltpu.VMEM((BLOCK, lw), bf16)] * 2,
        flops=nb * 2 * pair_flops,
        nbytes=nb * BLOCK * lw * 12,
        exps=nb * heads * BLOCK * SPAN,
    )

    halves = {}
    stacked = None
    for first in (2, 0):
        aliases = [] if stacked is None else [(array, n) for n, array in enumerate(stacked)]
        pos = lambda *tail, first=first: pl.BlockSpec(
            (1,) + tail, lambda g, t: (first + g, 0, 0)
        )
        blk = lambda *tail, first=first: pl.BlockSpec(
            (1,) + tail, lambda g, t: ((first + g) ^ t[0], 0, 0)
        )
        *stacked, halves[first] = call(
            functools.partial(state_kernel, scale, heads),
            (2,),
            (t_pre,),
            [
                (qkv, pl.BlockSpec((BLOCK, lw), lambda g, t, first=first: (first + g, 0))),
                (entry, full(NS, lw)),
                (before, blk(NS, lw)),
                (carry_rows, blk(1, lw)),
                (keep_rows, blk(1, lw)),
                (gate_row, full(1, lw)),
                (updates, pos(NS, lw)),
                (acc, blk(BLOCK, lw)),
                (ml, blk(BLOCK, 128)),
                (w_output, full(lw, width)),
            ],
            [
                ((nb, BLOCK, lw), bf16, pos(BLOCK, lw)),
                ((nb, BLOCK, 128), f32, pos(BLOCK, 128)),
                ((nb, NS, lw), bf16, pos(NS, lw)),
                ((nb, NS, lw), f32, blk(NS, lw)),
                ((2 * BLOCK, width), bf16, pl.BlockSpec((BLOCK, width), lambda g, t: (g, 0))),
            ],
            aliases,
            flops=2 * (4 * BLOCK * NS * lw + 2 * BLOCK * lw * width),
            nbytes=2 * BLOCK * (lw * 24 + width * 2),
            exps=2 * heads * BLOCK * NS,
        )
    mixed_all, stats_f, used_low, block_states = stacked

    def pair_sum(half):
        return (half[:BLOCK].astype(f32) + core(half[BLOCK:]).astype(f32)).astype(bf16)

    sum2 = pair_sum(halves[2])
    sum0 = pair_sum(halves[0])
    cross2 = cross(sum2)
    cross0 = cross(sum0)

    def norm_mlp(tok, mine, theirs):
        residual = tok.astype(f32) + (mine.astype(f32) + theirs.astype(f32))
        inverse = lax.rsqrt(jnp.mean(residual * residual, axis=-1, keepdims=True) + eps)
        return residual, inverse, (residual * inverse * gain_mlp).astype(bf16)

    residual0, inverse0, nm0 = norm_mlp(toks[0], sum0, cross2)
    residual2, inverse2, nm2 = norm_mlp(toks[2], sum2, cross0)
    nms = [nm0, core(nm0), nm2, core(nm2)]

    gacts = [nt(cot, w_return).astype(bf16) for cot in cots]
    stacked = None
    parts = []
    for r in range(nb):
        aliases = [] if stacked is None else [(array, n) for n, array in enumerate(stacked)]
        tile = 256
        steps = BLOCK // tile
        *stacked, part = call(
            mlp_kernel,
            (steps,),
            (),
            [
                (nms[r], pl.BlockSpec((tile, width), lambda g: (g, 0))),
                (gacts[r], pl.BlockSpec((tile, ff), lambda g: (g, 0))),
                (w_hidden, full(width, ff)),
            ],
            [
                (
                    (rows_all, ff),
                    bf16,
                    pl.BlockSpec((tile, ff), lambda g, r=r: (r * steps + g, 0)),
                ),
                (
                    (rows_all, ff),
                    bf16,
                    pl.BlockSpec((tile, ff), lambda g, r=r: (r * steps + g, 0)),
                ),
                ((BLOCK, width), bf16, pl.BlockSpec((tile, width), lambda g: (g, 0))),
            ],
            aliases,
            flops=4 * BLOCK * width * ff,
            nbytes=BLOCK * width * 10,
            exps=2 * BLOCK * ff,
        )
        parts.append(part)
    hidden_all, gpre_all = stacked

    back0 = (parts[0].astype(f32) + core(parts[1]).astype(f32)).astype(bf16)
    back2 = (parts[2].astype(f32) + core(parts[3]).astype(f32)).astype(bf16)
    cross0 = cross(back0)
    cross2 = cross(back2)

    def norm_mlp_back(cot, mine, theirs, residual, inverse):
        scaled = residual * inverse
        grad = (mine.astype(f32) + theirs.astype(f32)) * gain_mlp
        inner = jnp.mean(grad * scaled, axis=-1, keepdims=True)
        return cot.astype(f32) + inverse * (grad - scaled * inner)

    ga2 = norm_mlp_back(cots[2], back2, cross0, residual2, inverse2).astype(bf16)
    grad_residual = norm_mlp_back(cots[0], back0, cross2, residual0, inverse0)
    ga0 = grad_residual.astype(bf16)
    gas = [ga0, core(ga0), ga2, core(ga2)]

    mlp_part = nn(hidden_all, w_return).astype(bf16)
    mlp_parts = [mlp_part[r * BLOCK : (r + 1) * BLOCK] for r in range(nb)]
    far = mlp_parts[2].astype(f32) + core(mlp_parts[3]).astype(f32)
    mlp_out = (
        mlp_parts[0].astype(f32)
        + core(mlp_parts[1]).astype(f32)
        + cross(far.astype(bf16)).astype(f32)
    )
    result = (residual0 + mlp_out).astype(bf16)

    stacked = None
    for r in (2, 3, 0, 1):
        aliases = [] if stacked is None else [(array, n) for n, array in enumerate(stacked)]
        tile = 256
        steps = BLOCK // tile
        pos = lambda *tail, r=r: pl.BlockSpec((1,) + tail, lambda g: (r, g, 0))
        whole = lambda *tail, r=r: pl.BlockSpec((1,) + tail, lambda g: (r, 0, 0))
        stacked = call(
            functools.partial(state_back_kernel, scale, heads),
            (steps,),
            (),
            [
                (gas[r], pl.BlockSpec((tile, width), lambda g: (g, 0))),
                (w_output, full(lw, width)),
                (qkv, pl.BlockSpec((tile, lw), lambda g, r=r: (r * steps + g, 0))),
                (mixed_all, pos(tile, lw)),
                (used_low, whole(NS, lw)),
                (stats_f, pos(tile, 128)),
            ],
            [
                ((nb, BLOCK, lw), bf16, pos(tile, lw)),
                ((nb, BLOCK, 128), f32, pos(tile, 128)),
                ((nb, BLOCK, lw), f32, pos(tile, lw)),
                ((nb, NS, lw), f32, whole(NS, lw)),
            ],
            aliases,
            flops=2 * BLOCK * lw * width + 10 * BLOCK * NS * lw,
            nbytes=BLOCK * (width * 4 + lw * 16),
            exps=heads * BLOCK * NS,
        )
    gm_all, stats_b, dq_state, direct = stacked

    local_grad = jnp.zeros((NS, lw), f32)
    for j in reversed(range(nb)):
        local_grad = keeps[j] * (in_order(direct, j) + gates * local_grad)
    carried = jnp.zeros((NS, lw), f32)
    step = 1
    while step < groups:
        sent = (local_grad + factor_total * carried).astype(bf16)
        got = along(sent, -step).astype(f32)
        kept = keep_between(s_index + 1, s_index + step - 1)
        carried = (gate_power(nb * (step - 1)) * kept) * got + carried
        step *= 2

    turn = lambda j: nb - 1 - j
    at = lambda col: pl.BlockSpec((BLOCK, lw), lambda j, t: (turn(j) ^ t[0], col))
    prev = lambda col: pl.BlockSpec(
        (BLOCK, lw), lambda j, t: (jnp.maximum(turn(j) - 1, 0) ^ t[0], col)
    )
    pos = lambda *tail: pl.BlockSpec((1,) + tail, lambda j, t: (turn(j) ^ t[0], 0, 0))
    dq, dk, dv, back_k, back_v, bias_grad = call(
        functools.partial(window_back_kernel, scale, heads),
        (nb,),
        (t_pre,),
        [
            (qkv, at(0)),
            (qkv, at(1)),
            (qkv, at(2)),
            (qkv, prev(1)),
            (qkv, prev(2)),
            (edge, pl.BlockSpec((BLOCK, lw), lambda j, t: (0, 0))),
            (edge, pl.BlockSpec((BLOCK, lw), lambda j, t: (0, 1))),
            (id_cols, pl.BlockSpec((BLOCK, 1), lambda j, t: (turn(j), 0))),
            (id_rows, pl.BlockSpec((1, 1, BLOCK), lambda j, t: (turn(j), 0, 0))),
            (id_rows, pl.BlockSpec((1, 1, BLOCK), lambda j, t: (turn(j) + 1, 0, 0))),
            (bias, full(heads, TILE, SPAN)),
            (gm_all, pos(BLOCK, lw)),
            (stats_b, pos(BLOCK, 128)),
            (dq_state, pos(BLOCK, lw)),
        ],
        [
            ((rows_all, lw), bf16, pl.BlockSpec((BLOCK, lw), lambda j, t: (turn(j) ^ t[0], 0))),
            ((nb, BLOCK, lw), f32, pos(BLOCK, lw)),
            ((nb, BLOCK, lw), f32, pos(BLOCK, lw)),
            ((BLOCK, lw), bf16, full(BLOCK, lw)),
            ((BLOCK, lw), bf16, full(BLOCK, lw)),
            ((heads, TILE, SPAN), f32, full(heads, TILE, SPAN)),
        ],
        scratch=[pltpu.VMEM((BLOCK, lw), bf16)] * 2 + [pltpu.VMEM((BLOCK, lw), f32)] * 4,
        flops=nb * 5 * pair_flops,
        nbytes=nb * BLOCK * lw * 24,
        exps=nb * heads * BLOCK * SPAN,
    )
    next_k = along(back_k, -1)
    next_v = along(back_v, -1)
    (bias_line,) = call(
        bias_sum_kernel,
        (1,),
        (),
        [(bias_grad, full(heads, TILE, SPAN))],
        [((heads, SPAN), f32, full(heads, SPAN))],
    )
    bias_local = jnp.dot(bias_line, onehot, precision=lax.Precision.HIGHEST)

    blk = lambda *tail: pl.BlockSpec((1,) + tail, lambda j, t: (turn(j), 0, 0))
    row = lambda cols: pl.BlockSpec((BLOCK, cols), lambda j, t: (turn(j) ^ t[0], 0))
    dkv, parts, grad_sq, gate_sum = call(
        functools.partial(update_back_kernel, scale, heads),
        (nb,),
        (t_pre,),
        [
            (carried, full(NS, lw)),
            (direct, pos(NS, lw)),
            (entry, full(NS, lw)),
            (before, blk(NS, lw)),
            (carry_rows, blk(1, lw)),
            (keep_rows, blk(1, lw)),
            (gate_row, full(1, lw)),
            (qkv, at(1)),
            (qkv, at(2)),
            (state_queries, full(NS, lw)),
            (lse_u, pos(NS, 128)),
            (updates, pos(NS, lw)),
            (dq, row(lw)),
            (dk, pos(BLOCK, lw)),
            (dv, pos(BLOCK, lw)),
            (next_k, full(BLOCK, lw)),
            (next_v, full(BLOCK, lw)),
            (w_joined, full(width, 3 * lw)),
        ],
        [
            ((rows_all, 2 * lw), bf16, row(2 * lw)),
            ((rows_all, width), bf16, row(width)),
            ((NS, lw), f32, full(NS, lw)),
            ((1, lw), f32, full(1, lw)),
        ],
        scratch=[pltpu.VMEM((NS, lw), f32)],
        flops=nb * (10 * NS * BLOCK * lw + 6 * BLOCK * lw * width),
        nbytes=nb * BLOCK * (lw * 30 + width * 2),
        exps=nb * heads * NS * BLOCK,
    )
    pieces = [parts[r * BLOCK : (r + 1) * BLOCK] for r in range(nb)]
    far = pieces[2].astype(f32) + core(pieces[3]).astype(f32)
    grad_normed = (
        pieces[0].astype(f32)
        + core(pieces[1]).astype(f32)
        + cross(far.astype(bf16)).astype(f32)
    )
    token_float = tokens.astype(f32)
    inverse = lax.rsqrt(jnp.mean(token_float * token_float, axis=-1, keepdims=True) + eps)
    scaled = token_float * inverse
    grad_scaled = grad_normed * gain_attn
    inner = jnp.mean(grad_scaled * scaled, axis=-1, keepdims=True)
    grad_tokens = grad_residual + inverse * (grad_scaled - scaled * inner)

    cot_all = jnp.concatenate(cots)
    nm_all = jnp.concatenate(nms)
    ga_all = jnp.concatenate(gas)
    grad_hidden = tn(nm_all, gpre_all)
    grad_return_t = tn(cot_all, hidden_all)
    grad_output_t = tn(ga_all, mixed_all.reshape(rows_all, lw))
    gain_mlp_part = jnp.sum(grad_hidden * w_hidden.astype(f32), axis=1) / gain_mlp
    early = jnp.concatenate(
        [grad_hidden.astype(bf16), grad_return_t.astype(bf16), grad_output_t.astype(bf16)], axis=1
    )
    early = lax.psum_scatter(early, "seq", scatter_dimension=0, tiled=True).astype(f32)
    hidden_sent = early[:, :ff]
    return_sent = early[:, ff : 2 * ff].T
    output_sent = early[:, 2 * ff :].T

    grad_q = tn(normed_all, dq)
    grad_kv = tn(normed_all, dkv)
    gain_attn_part = (
        jnp.sum(grad_q * w_query.astype(f32), axis=1)
        + jnp.sum(grad_kv * w_joined[:, lw:].astype(f32), axis=1)
    ) / gain_attn
    share = NS // groups
    state_grads = jnp.concatenate([grad_sq, prefix_factor * local_grad], axis=1).astype(bf16)
    late = jnp.concatenate([grad_q.astype(bf16), grad_kv.astype(bf16)], axis=1)
    late = late.reshape(groups, width // groups, 3 * lw)
    late = lax.all_to_all(late, "seq", 0, 0, tiled=True)
    joined_sent = jnp.sum(late.astype(f32), axis=0)
    state_grads = state_grads.reshape(groups, share, 2 * lw)
    state_grads = lax.all_to_all(state_grads, "seq", 0, 0, tiled=True)
    state_grads = jnp.sum(state_grads.astype(f32), axis=0)

    bias_full = lax.dynamic_update_slice(
        jnp.zeros((H, BUCKETS), f32), bias_local, (t_index * heads, 0)
    )
    gate_full = lax.dynamic_update_slice(
        jnp.zeros((D,), f32), gate_sum[0] * gates * (1.0 - gates), (t_index * lw,)
    )
    small = jnp.concatenate(
        [gain_attn_part, gain_mlp_part, gate_full, bias_full.reshape(-1)]
    ).reshape(-1, 128)
    small = small + core(small)
    small = small + cross(small)
    step = 1
    while step < groups:
        small = small + lax.ppermute(small, "seq", [(i, i ^ step) for i in range(groups)])
        step *= 2
    small = small.reshape(-1)
    return (
        result,
        block_states,
        grad_tokens,
        state_grads[:, lw:],
        small[:D],
        joined_sent[:, :lw],
        joined_sent[:, lw : 2 * lw],
        joined_sent[:, 2 * lw :],
        output_sent,
        small[3 * D :].reshape(H, BUCKETS),
        state_grads[:, :lw],
        small[2 * D : 3 * D],
        small[D : 2 * D],
        hidden_sent,
        return_sent,
    )


def solution(mesh):
    return jax.shard_map(
        local,
        mesh=mesh,
        in_specs=(
            P(("seq", "tp"), None),
            P("seq"),
            P("seq"),
            P(None, "tp"),
            P(),
            P(None, "tp"),
            P(None, "tp"),
            P(None, "tp"),
            P("tp", None),
            P("tp", None),
            P(None, "tp"),
            P("tp"),
            P(),
            P(None, "tp"),
            P("tp", None),
            P(("seq", "tp"), None),
        ),
        out_specs=(
            P(("seq", "tp"), None),
            P("seq", None, "tp"),
            P(("seq", "tp"), None),
            P("seq", "tp"),
            P(),
            P("seq", "tp"),
            P("seq", "tp"),
            P("seq", "tp"),
            P("tp", "seq"),
            P(),
            P("seq", "tp"),
            P(),
            P(),
            P("seq", "tp"),
            P("tp", "seq"),
        ),
        check_vma=False,
    )
```

time: 1270 us -> 581 us (0.46)
  waiting for transfers between devices: 659 us -> 193 us
  other arithmetic: 222 us -> 68.3 us
  matrix products: 197 us -> 45.4 us
  Pallas kernels: 0 us -> 141 us
  blocking collectives: 78.6 us -> 0 us
  starting transfers between devices: 14.1 us -> 64.3 us
  local copies, waits for them, and re-layouts: 67.7 us -> 43.5 us
    reduce_scatter x9 -> x0, waiting for transfers between devices: 494 us -> none  [the longest x1 92.9 us: local(): lax.psum_scatter(grad_return_sum, 'seq', scatter_dimension=1, tiled=True)]
    ppermute x5 -> x42, waiting for transfers between devices: 0.01 us -> 187 us  [the longest x9 112 us: cross(): return lax.ppermute(value, 'tp', [(i, i ^ 2) for i in range(nb)])]
    pallas_call x0 -> x19, Pallas kernels: none -> 141 us  [call(): pl.pallas_call(body, out_shape=[jax.ShapeDtypeStruct(shape, dtype) for sh...]
    dot_general x56 -> x12, matrix products: 186 us -> 45.4 us  [the longest x5 23.1 us: tn(): lax.dot_general(a, b, (((0,), (0,)), ((), ())), preferred_element_type=f32)]
    all_gather x6 -> x0, waiting for transfers between devices: 99.4 us -> none  [the longest x1 34.6 us: local(): piece = lax.all_gather(grad_attn_low, 'tp', axis=0, tiled=True)]
    unnamed x17 -> x2, waiting for transfers between devices: 65.5 us -> 0.02 us
    ppermute x5 -> x42, starting transfers between devices: 12.8 us -> 56.4 us  [the longest x10 29 us: along(): return lax.ppermute(value, 'seq', pairs)]
    add x19 -> x9, other arithmetic: 48.9 us -> 7.35 us  [the longest x1 4 us: local(): grad_tokens = grad_residual + inverse * (grad_scaled - scaled * inner)]
  transfers between devices with their start and end apart: 21 -> 45, of which waited for: 14 -> 16; matrix products, arithmetic and copies ran while one was open for 22% -> 23% of each run, Pallas kernels for 0% -> 22%
where the time goes in v1:
time: 581 us; the launch traced here: 571 us
  waiting for transfers between devices  193 us (33%)
  Pallas kernels  141 us (24%)
  other arithmetic  68.3 us (12%)
  starting transfers between devices  64.3 us (11%)
  matrix products  45.4 us (8%)
  local copies, waits for them, and re-layouts  43.5 us (7%)
  between operations  15.5 us (3%)
    pallas_call x19, Pallas kernels, call(): pl.pallas_call(body, out_shape=[jax.ShapeDtypeStruct(shape, dtype) for sh...  141 us
    ppermute x9, waiting for transfers between devices, cross(): return lax.ppermute(value, 'tp', [(i, i ^ 2) for i in range(nb)])  112 us
    ppermute x10, waiting for transfers between devices, along(): return lax.ppermute(value, 'seq', pairs)  47.8 us
    ppermute x10, starting transfers between devices, along(): return lax.ppermute(value, 'seq', pairs)  29 us
    unnamed x128, local copies, waits for them, and re-layouts  26.3 us
    dot_general x5, matrix products, tn(): lax.dot_general(a, b, (((0,), (0,)), ((), ())), preferred_element_type=f32)  23.1 us
    ppermute x3, waiting for transfers between devices, local(): lax.ppermute(small, 'seq', [(i, i ^ step) for i in range(groups)])  22.6 us
    dot_general x4, matrix products, nt(): lax.dot_general(a, b, (((1,), (1,)), ((), ())), preferred_element_type=f32)  13.3 us
  transfers between devices with their start and end apart: 45, of which 16 were waited for; matrix products, arithmetic and copies ran while one was open for 23% of the time, Pallas kernels for 22%

profile of v1, /device:TPU:0, one launch (start us, length us, event | category | flops | bytes accessed | tf_op | source)
XLA Modules:
  0.0 571.2 jit_solution(15587556081270509824)
XLA Ops:
  20.8 5.2 shard_map.289
  38.6 5.7 %broadcast_multiply_fusion.3 = (f32[256]{0:T(256)S(1)}, f32[256]{0:T(256)S(1)}, f32[256]{0:T(256)S(1)}, f32[256]{0:T(256)S(1)}, f32[256]{0:T(256)}, /*index=5*/f...) fusion(f32[]{:T(128)} %get-tuple-element.197, ...), kind=kLoop, calls=%fused_computation.159 | loop fusion | flops 5888 | bytes 14371 | tf_op jit(solution)/shard_map/mul | solution.py:693
  48.9 5.1 shard_map.290
  54.0 5.1 shard_map.291
  59.1 5.1 shard_map.292
  70.3 4.4 collective-permute-start.9
  75.5 6.7 %collective-permute-start.7 = (bf16[512,256]{1,0:T(8,128)(2,1)S(1)}, bf16[512,256]{1,0:T(8,128)(2,1)S(1)}, u32[]{:S(2)}, u32[]{:S(2)}) collective-permute-start(bf16[512,256]{1,0:T(8,128)(2,1)S(1)} %add_convert_fusion.12), channel_id=1, source_target_pairs={{0,8},{4,12},{8,16},{12,20},{16,24},{20,28},{1,9},{5,13},{9,17},{1... | collective-permute-start | bytes 786440 | tf_op jit(solution)/shard_map/ppermute | solution.py:391
  82.4 4.8 collective-permute-done.7
  88.0 5.6 collective-permute-start.8
  95.9 13.6 %shard_map.294 = (f32[4,512,256]{2,1,0:T(8,128)}, f32[4,512,128]{2,1,0:T(8,128)}) custom-call(s32[1]{0:T(128)} %bitcast.refs_0_, bf16[2048,768]{1,0:T(8,128)(2,1)} %get-tuple-element.93.refs_1_.refs_2_.refs_3_.refs_4_.refs_5_.refs_8_.refs_9_, bf16[2048,768]{1,0:T(8,128)(2,1)} %get-tuple-element.93.refs_1_.refs_2_.refs_3_.refs_4_.refs_5_.refs_8_.refs_9_, ...), custom_call_target="tpu_custom_call" | custom-call | flops 1342177280 | bytes 6291456 | tf_op jit(solution)/shard_map/pallas_call | solution.py:54
  111.8 8.6 %shard_map.295 = (bf16[4,512,256]{2,1,0:T(8,128)(2,1)}, f32[4,512,128]{2,1,0:T(8,128)}, bf16[4,512,256]{2,1,0:T(8,128)(2,1)}, f32[4,512,256]{2,1,0:T(8,128)}, bf16[1024,1024]{1,0:T(8,128)(2,1)}) custom-call(s32[1]{0:T(128)} %bitcast.refs_0_, bf16[2048,768]{1,0:T(8,128)(2,1)} %get-tuple-element.93.refs_1_.refs_2_.refs_3_.refs_4_.refs_5_.refs_8_.refs_9_, ...), custom_call_target="tpu_custom_call" | custom-call | flops 1073741824 | bytes 8388608 | tf_op jit(solution)/shard_map/pallas_call | solution.py:54
  121.8 8.6 %shard_map.296 = (bf16[4,512,256]{2,1,0:T(8,128)(2,1)}, f32[4,512,128]{2,1,0:T(8,128)}, bf16[4,512,256]{2,1,0:T(8,128)(2,1)}, f32[4,512,256]{2,1,0:T(8,128)}, bf16[1024,1024]{1,0:T(8,128)(2,1)}) custom-call(s32[1]{0:T(128)} %bitcast.refs_0_, ...), custom_call_target="tpu_custom_call", output_to_operand_aliasing={{0}: (11, {}), {1}: (12, {}), {2}: (13, {}), {3}: (14, {})} | custom-call | flops 1073741824 | bytes 8388608 | tf_op jit(solution)/shard_map/pallas_call | solution.py:54
  135.9 23.9 %collective-permute-done.13 = bf16[512,1024]{1,0:T(8,128)(2,1)S(1)} collective-permute-done((bf16[512,1024]{1,0:T(8,128)(2,1)S(1)}, bf16[512,1024]{1,0:T(8,128)(2,1)S(1)}, u32[]{:S(2)}, u32[]{:S(2)}) %collective-permute-start.13) | collective-permute-done | bytes 1048608 | tf_op jit(solution)/shard_map/ppermute | solution.py:387
  162.1 4.1 copy.84
  166.2 3.6 convolution_convert_fusion.1.refs_1_
  169.9 12.6 %collective-permute-done.16 = bf16[512,1024]{1,0:T(8,128)(2,1)} collective-permute-done((bf16[512,1024]{1,0:T(8,128)(2,1)}, bf16[512,1024]{1,0:T(8,128)(2,1)}, u32[]{:S(2)}, u32[]{:S(2)}) %collective-permute-start.16) | collective-permute-done | bytes 1048608 | tf_op jit(solution)/shard_map/ppermute | solution.py:387
  182.5 21.9 %collective-permute-done.14 = bf16[512,1024]{1,0:T(8,128)(2,1)} collective-permute-done((bf16[512,1024]{1,0:T(8,128)(2,1)}, bf16[512,1024]{1,0:T(8,128)(2,1)}, u32[]{:S(2)}, u32[]{:S(2)}) %collective-permute-start.14) | collective-permute-done | bytes 1048608 | tf_op jit(solution)/shard_map/ppermute | solution.py:387
  209.6 3.9 convolution_convert_fusion.3.refs_1_
  220.3 7.0 %shard_map.297 = (bf16[2048,1024]{1,0:T(8,128)(2,1)}, bf16[2048,1024]{1,0:T(8,128)(2,1)}, bf16[512,1024]{1,0:T(8,128)(2,1)}) custom-call(bf16[512,1024]{1,0:T(8,128)(2,1)} %get-tuple-element.246.refs_0_, bf16[512,1024]{1,0:T(8,128)(2,1)} %convolution_convert_fusion.1.refs_1_, bf16[1024,1024]{1,0:T(8,128)(2,1)} %refs_2_.7), custom_call_target="tpu_custom_call" | custom-call | flops 2147483648 | bytes 5242880 | tf_op jit(solution)/shard_map/pallas_call | solution.py:54
  227.3 7.0 %shard_map.298 = (bf16[2048,1024]{1,0:T(8,128)(2,1)}, bf16[2048,1024]{1,0:T(8,128)(2,1)}, bf16[512,1024]{1,0:T(8,128)(2,1)}) custom-call(bf16[512,1024]{1,0:T(8,128)(2,1)} %collective-permute-done.18.refs_0_, bf16[512,1024]{1,0:T(8,128)(2,1)} %convolution_convert_fusion.2.refs_1_, ...), custom_call_target="tpu_custom_call", output_to_operand_aliasing={{0}: (3, {}), {1}: (4, {})} | custom-call | flops 2147483648 | bytes 5242880 | tf_op jit(solution)/shard_map/pallas_call | solution.py:54
  234.7 7.1 %shard_map.299 = (bf16[2048,1024]{1,0:T(8,128)(2,1)}, bf16[2048,1024]{1,0:T(8,128)(2,1)}, bf16[512,1024]{1,0:T(8,128)(2,1)}) custom-call(bf16[512,1024]{1,0:T(8,128)(2,1)} %copy-done.18, bf16[512,1024]{1,0:T(8,128)(2,1)} %convolution_convert_fusion.3.refs_1_, bf16[1024,1024]{1,0:T(8,128)(2,1)} %refs_2_.7, ...), custom_call_target="tpu_custom_call", output_to_operand_aliasing={{0}: (3, {}), {1}: (4, {})} | custom-call | flops 2147483648 | bytes 5242880 | tf_op jit(solution)/shard_map/pallas_call | solution.py:54
  241.8 7.5 %shard_map.300 = (bf16[2048,1024]{1,0:T(8,128)(2,1)}, bf16[2048,1024]{1,0:T(8,128)(2,1)}, bf16[512,1024]{1,0:T(8,128)(2,1)}) custom-call(bf16[512,1024]{1,0:T(8,128)(2,1)} %collective-permute-done.15.refs_0_, bf16[512,1024]{1,0:T(8,128)(2,1)} %convolution_convert_fusion.4.refs_1_, ...), custom_call_target="tpu_custom_call", output_to_operand_aliasing={{0}: (3, {}), {1}: (4, {})} | custom-call | flops 2147483648 | bytes 5242880 | tf_op jit(solution)/shard_map/pallas_call | solution.py:54
  249.5 6.9 %convolution_convert_fusion = bf16[2048,1024]{1,0:T(8,128)(2,1)S(1)} fusion(bf16[2048,1024]{1,0:T(8,128)(2,1)} %get-tuple-element.109, bf16[1024,1024]{1,0:T(8,128)(2,1)S(1)} %copy-done), kind=kOutput, calls=%fused_computation.26 | convolution fusion | flops 4297064448 | bytes 10485760 | tf_op jit(solution)/shard_map/dot_general | solution.py:31
  262.8 6.8 %fusion.31 = bf16[1024,1024]{0,1:T(8,128)(2,1)S(1)} fusion(bf16[2048,1024]{1,0:T(8,128)(2,1)S(1)} %copy-done.3, bf16[512,1024]{1,0:T(8,128)(2,1)} %copy-done.57, bf16[512,1024]{1,0:T(8,128)(2,1)} %collective-permute-done.16, bf16[512,1024]{1,0:T(8,128)(2,1)} %collective-permute-done.19, bf16[512,1024]{1,0:T(8,128)(2,1)} %param.33), kind=kOutput, calls=%fused_computation.59 | convolution fusion | flops 4312793088 | bytes 10485760 | tf_op jit(solution)/shard_map/dot_general | solution.py:39
  270.7 15.6 %collective-permute-done.27 = bf16[512,1024]{1,0:T(8,128)(2,1)S(1)} collective-permute-done((bf16[512,1024]{1,0:T(8,128)(2,1)S(1)}, bf16[512,1024]{1,0:T(8,128)(2,1)S(1)}, u32[]{:S(2)}, u32[]{:S(2)}) %collective-permute-start.27) | collective-permute-done | bytes 1048608 | tf_op jit(solution)/shard_map/ppermute | solution.py:387
  286.3 22.5 %collective-permute-done.25 = bf16[512,1024]{1,0:T(8,128)(2,1)S(1)} collective-permute-done((bf16[512,1024]{1,0:T(8,128)(2,1)S(1)}, bf16[512,1024]{1,0:T(8,128)(2,1)S(1)}, u32[]{:S(2)}, u32[]{:S(2)}) %collective-permute-start.25) | collective-permute-done | bytes 1048608 | tf_op jit(solution)/shard_map/ppermute | solution.py:387
  308.7 3.6 fusion.30
  315.2 15.5 %collective-permute-done.22 = bf16[512,1024]{1,0:T(8,128)(2,1)S(1)} collective-permute-done((bf16[512,1024]{1,0:T(8,128)(2,1)S(1)}, bf16[512,1024]{1,0:T(8,128)(2,1)S(1)}, u32[]{:S(2)}, u32[]{:S(2)}) %collective-permute-start.22) | collective-permute-done | bytes 1048608 | tf_op jit(solution)/shard_map/ppermute | solution.py:387
  330.7 4.9 fusion.76
  335.7 7.1 %fusion.77 = (bf16[1024,1024]{0,1:T(8,128)(2,1)S(1)}, f32[1024]{0:T(1024)S(1)}) fusion(bf16[1024,1024]{0,1:T(8,128)(2,1)S(1)} %copy-done.24, bf16[2048,1024]{1,0:T(8,128)(2,1)S(1)} %copy-done.4, bf16[512,1024]{1,0:T(8,128)(2,1)} %collective-permute-done.15.refs_0_, bf16[512,1024]{1,0:T(8,128)(2,1)S(1)} %copy-done.19, ...), kind=kOutput, calls=%fused_computation.187 | convolution fusion | flops 4315937792 | bytes 12587008 | tf_op jit(solution)/shard_map/dot_general | solution.py:39
  347.0 6.7 %copy.91 = bf16[1024,2304]{1,0:T(8,128)(2,1)} copy(bf16[1024,2304]{0,1:T(8,128)(2,1)} %pad_maximum_fusion) | data formatting | bytes 9437184
  357.8 5.8 %shard_map.301 = (bf16[4,512,256]{2,1,0:T(8,128)(2,1)}, f32[4,512,128]{2,1,0:T(8,128)}, f32[4,512,256]{2,1,0:T(8,128)}, f32[4,512,256]{2,1,0:T(8,128)}) custom-call(bf16[512,1024]{1,0:T(8,128)(2,1)} %copy-done.21, bf16[256,1024]{1,0:T(8,128)(2,1)} %refs_1_.7, bf16[2048,768]{1,0:T(8,128)(2,1)} %get-tuple-element.93.refs_1_.refs_2_.refs_3_.refs_4_.refs_5_.refs_8_.refs_9_, ...), custom_call_target="tpu_custom_call" | custom-call | flops 939524096 | bytes 4194304 | tf_op jit(solution)/shard_map/pallas_call | solution.py:54
  363.6 6.1 %shard_map.302 = (bf16[4,512,256]{2,1,0:T(8,128)(2,1)}, f32[4,512,128]{2,1,0:T(8,128)}, f32[4,512,256]{2,1,0:T(8,128)}, f32[4,512,256]{2,1,0:T(8,128)}) custom-call(bf16[512,1024]{1,0:T(8,128)(2,1)} %copy-done.31, bf16[256,1024]{1,0:T(8,128)(2,1)} %refs_1_.7, ...), custom_call_target="tpu_custom_call", output_to_operand_aliasing={{0}: (6, {}), {1}: (7, {}), {2}: (8, {}), {3}: (9, {})} | custom-call | flops 939524096 | bytes 4194304 | tf_op jit(solution)/shard_map/pallas_call | solution.py:54
  369.7 5.9 %shard_map.303 = (bf16[4,512,256]{2,1,0:T(8,128)(2,1)}, f32[4,512,128]{2,1,0:T(8,128)}, f32[4,512,256]{2,1,0:T(8,128)}, f32[4,512,256]{2,1,0:T(8,128)}) custom-call(bf16[512,1024]{1,0:T(8,128)(2,1)} %copy-done.20, bf16[256,1024]{1,0:T(8,128)(2,1)} %refs_1_.7, ...), custom_call_target="tpu_custom_call", output_to_operand_aliasing={{0}: (6, {}), {1}: (7, {}), {2}: (8, {}), {3}: (9, {})} | custom-call | flops 939524096 | bytes 4194304 | tf_op jit(solution)/shard_map/pallas_call | solution.py:54
  375.6 5.8 %shard_map.304 = (bf16[4,512,256]{2,1,0:T(8,128)(2,1)}, f32[4,512,128]{2,1,0:T(8,128)}, f32[4,512,256]{2,1,0:T(8,128)}, f32[4,512,256]{2,1,0:T(8,128)}) custom-call(bf16[512,1024]{1,0:T(8,128)(2,1)} %copy-done.32, bf16[256,1024]{1,0:T(8,128)(2,1)} %refs_1_.7, ...), custom_call_target="tpu_custom_call", output_to_operand_aliasing={{0}: (6, {}), {1}: (7, {}), {2}: (8, {}), {3}: (9, {})} | custom-call | flops 939524096 | bytes 4194304 | tf_op jit(solution)/shard_map/pallas_call | solution.py:54
  381.5 5.2 add_convert_fusion.10
  388.0 16.7 %shard_map.305 = (bf16[2048,256]{1,0:T(8,128)(2,1)}, f32[4,512,256]{2,1,0:T(8,128)}, f32[4,512,256]{2,1,0:T(8,128)}, bf16[512,256]{1,0:T(8,128)(2,1)}, bf16[512,256]{1,0:T(8,128)(2,1)}, /*index=5*/f32[2,128,640]{2,1,0:T(8,128)}) custom-call(s32[1]{0:T(128)} %bitcast.refs_0_, ...), custom_call_target="tpu_custom_call" | custom-call | flops 3355443200 | bytes 12582912 | tf_op jit(solution)/shard_map/pallas_call | solution.py:54
  412.9 21.0 %collective-permute-done.30 = bf16[512,256]{1,0:T(8,128)(2,1)S(1)} collective-permute-done((bf16[512,256]{1,0:T(8,128)(2,1)S(1)}, bf16[512,256]{1,0:T(8,128)(2,1)S(1)}, u32[]{:S(2)}, u32[]{:S(2)}) %collective-permute-start.30) | collective-permute-done | bytes 262176 | tf_op jit(solution)/shard_map/ppermute | solution.py:391
  443.4 22.0 %collective-permute-done.31 = bf16[512,256]{1,0:T(8,128)(2,1)S(1)} collective-permute-done((bf16[512,256]{1,0:T(8,128)(2,1)}, bf16[512,256]{1,0:T(8,128)(2,1)S(1)}, u32[]{:S(2)}, u32[]{:S(2)}) %collective-permute-start.31) | collective-permute-done | bytes 262176 | tf_op jit(solution)/shard_map/ppermute | solution.py:391
  467.0 16.5 %shard_map.306 = (bf16[2048,512]{1,0:T(8,128)(2,1)}, bf16[2048,1024]{1,0:T(8,128)(2,1)}, f32[512,256]{1,0:T(8,128)}, f32[1,256]{1,0:T(1,128)}) custom-call(s32[1]{0:T(128)} %bitcast.refs_0_, f32[512,256]{1,0:T(8,128)} %multiply_add_fusion.1.refs_1_, f32[4,512,256]{2,1,0:T(8,128)} %get-tuple-element.130.refs_2_, f32[512,256]{1,0:T(8,128)} %add_add_fusion.1.refs_2_.refs_3_, ...), custom_call_target="tpu_custom_call" | custom-call | flops 5905580032 | bytes 19922944 | tf_op jit(solution)/shard_map/pallas_call | solution.py:54
  492.3 4.1 fusion.80
  497.9 5.8 %all-to-all-done = bf16[8,64,512]{2,1,0:T(8,128)(2,1)S(1)} async-done(((bf16[8,64,512]{2,1,0:T(8,128)(2,1)}), bf16[8,64,512]{2,1,0:T(8,128)(2,1)S(1)}, u32[]{:S(2)}, u32[]{:S(2)}) %all-to-all-start) | async-done | bytes 524320 | tf_op jit(solution)/shard_map/all_to_all | solution.py:825
  503.8 4.3 all-to-all-start.1
  516.1 4.2 collective-permute-done.39
  522.5 11.2 %collective-permute-done.40 = f32[26,128]{1,0:T(8,128)S(1)} collective-permute-done((f32[26,128]{1,0:T(8,128)S(1)}, f32[26,128]{1,0:T(8,128)S(1)}, u32[]{:S(2)}, u32[]{:S(2)}) %collective-permute-start.40) | collective-permute-done | bytes 13344 | tf_op jit(solution)/shard_map/ppermute | solution.py:841
  533.6 4.4 collective-permute-start.41
  538.0 7.3 %collective-permute-done.41 = f32[26,128]{1,0:T(8,128)S(1)} collective-permute-done((f32[26,128]{1,0:T(8,128)S(1)}, f32[26,128]{1,0:T(8,128)S(1)}, u32[]{:S(2)}, u32[]{:S(2)}) %collective-permute-start.41) | collective-permute-done | bytes 13344 | tf_op jit(solution)/shard_map/ppermute | solution.py:841
  550.1 4.0 fusion.29
  (291 shorter events, 138.7 us)
Async XLA Ops:
  7.2 159.0 %copy-start = (bf16[1024,1024]{1,0:T(8,128)(2,1)S(1)}, bf16[1024,1024]{1,0:T(8,128)(2,1)}, u32[]{:S(2)}) copy-start(bf16[1024,1024]{1,0:T(8,128)(2,1)} %param.32) | copy-start | bytes 6291460
  7.2 550.8 %reduce-scatter.4.cloned.1.call-start = ((), (), s32[]{:S(2)}) async-start(), calls=%async_computation.3 | async-start | bytes 5308416
  7.3 41.6 %collective-permute-start.2 = (bf16[512,1024]{1,0:T(8,128)(2,1)}, bf16[512,1024]{1,0:T(8,128)(2,1)}, u32[]{:S(2)}, u32[]{:S(2)}) collective-permute-start(bf16[512,1024]{1,0:T(8,128)(2,1)} %refs_0_.1), channel_id=1, source_target_pairs={{0,1},{1,0},{2,3},{3,2},{4,5},{5,4},{6,7},{7,6},{8,9},{9,8},{10,11... | collective-permute-start | bytes 3145736 | tf_op jit(solution)/shard_map/ppermute | solution.py:384
  7.8 37.2 %collective-permute-start = (bf16[512,1024]{1,0:T(8,128)(2,1)}, bf16[512,1024]{1,0:T(8,128)(2,1)S(1)}, u32[]{:S(2)}, u32[]{:S(2)}) collective-permute-start(bf16[512,1024]{1,0:T(8,128)(2,1)} %refs_0_.1), channel_id=1, source_target_pairs={{0,2},{1,3},{2,0},{3,1},{4,6},{5,7},{6,4},{7,5},{8,10},{9,11},{10,... | collective-permute-start | bytes 3145736 | tf_op jit(solution)/shard_map/ppermute | solution.py:387
  11.1 34.6 %collective-permute-start.10 = (s32[512]{0:T(512)S(1)}, s32[512]{0:T(512)S(1)}, u32[]{:S(2)}, u32[]{:S(2)}) collective-permute-start(s32[512]{0:T(512)S(1)} %slice.117), channel_id=1, source_target_pairs={{0,4},{4,8},{8,12},{12,16},{16,20},{20,24},{24,28},{1,5},{5,9},{9,... | collective-permute-start | bytes 6152 | tf_op jit(solution)/shard_map/ppermute | solution.py:391
  14.5 13.8 %collective-permute-start.3 = (s32[1,4]{1,0:T(1,128)}, s32[1,4]{1,0:T(1,128)S(1)}, u32[]{:S(2)}, u32[]{:S(2)}) collective-permute-start(s32[1,4]{1,0:T(1,128)} %bitcast.140), channel_id=1, source_target_pairs={{0,4},{4,0},{8,12},{12,8},{16,20},{20,16},{24,28},{28,24},{1,5},{5... | collective-permute-start | bytes 56 | tf_op jit(solution)/shard_map/ppermute | solution.py:404
  28.4 3.6 collective-permute-start.4
  32.0 4.5 collective-permute-start.5
  45.0 14.0 %collective-permute-start.1 = (bf16[512,1024]{1,0:T(8,128)(2,1)S(1)}, bf16[512,1024]{1,0:T(8,128)(2,1)}, u32[]{:S(2)}, u32[]{:S(2)}) collective-permute-start(bf16[512,1024]{1,0:T(8,128)(2,1)S(1)} %collective-permute-done.refs_0_), channel_id=1, source_target_pairs={{0,1},{1,0},{2,3},{3,2},{4,5},{5,4},{6,7},{7,6},{8,9},{9,8},{10,11... | collective-permute-start | bytes 3145736 | tf_op jit(solution)/shard_map/ppermute | solution.py:384
  66.1 8.7 %collective-permute-start.6 = (bf16[512,256]{1,0:T(8,128)(2,1)S(1)}, bf16[512,256]{1,0:T(8,128)(2,1)S(1)}, u32[]{:S(2)}, u32[]{:S(2)}) collective-permute-start(bf16[512,256]{1,0:T(8,128)(2,1)S(1)} %get-tuple-element.217), channel_id=1, source_target_pairs={{0,4},{4,8},{8,12},{12,16},{16,20},{20,24},{24,28},{1,5},{5,9},{9,... | collective-permute-start | bytes 786440 | tf_op jit(solution)/shard_map/ppermute | solution.py:391
  70.3 24.8 %collective-permute-start.9 = (bf16[512,512]{1,0:T(8,128)(2,1)S(1)}, bf16[512,512]{1,0:T(8,128)(2,1)S(1)}, u32[]{:S(2)}, u32[]{:S(2)}) collective-permute-start(bf16[512,512]{1,0:T(8,128)(2,1)S(1)} %constant_dynamic-slice_fusion.4), channel_id=1, source_target_pairs={{0,4},{4,8},{8,12},{12,16},{16,20},{20,24},{24,28},{1,5},{5,9},{9,... | collective-permute-start | bytes 1572872 | tf_op jit(solution)/shard_map/ppermute | solution.py:391
  75.5 11.6 %collective-permute-start.7 = (bf16[512,256]{1,0:T(8,128)(2,1)S(1)}, bf16[512,256]{1,0:T(8,128)(2,1)S(1)}, u32[]{:S(2)}, u32[]{:S(2)}) collective-permute-start(bf16[512,256]{1,0:T(8,128)(2,1)S(1)} %add_convert_fusion.12), channel_id=1, source_target_pairs={{0,8},{4,12},{8,16},{12,20},{16,24},{20,28},{1,9},{5,13},{9,17},{1... | collective-permute-start | bytes 786440 | tf_op jit(solution)/shard_map/ppermute | solution.py:391
  88.0 21.5 %collective-permute-start.8 = (bf16[512,256]{1,0:T(8,128)(2,1)S(1)}, bf16[512,256]{1,0:T(8,128)(2,1)S(1)}, u32[]{:S(2)}, u32[]{:S(2)}) collective-permute-start(bf16[512,256]{1,0:T(8,128)(2,1)S(1)} %add_convert_fusion.11), channel_id=1, source_target_pairs={{0,16},{4,20},{8,24},{12,28},{1,17},{5,21},{9,25},{13,29},{2,18},{... | collective-permute-start | bytes 786440 | tf_op jit(solution)/shard_map/ppermute | solution.py:391
  121.7 10.7 %collective-permute-start.12 = (bf16[512,1024]{1,0:T(8,128)(2,1)S(1)}, bf16[512,1024]{1,0:T(8,128)(2,1)S(1)}, u32[]{:S(2)}, u32[]{:S(2)}) collective-permute-start(bf16[512,1024]{1,0:T(8,128)(2,1)S(1)} %slice.124), channel_id=1, source_target_pairs={{0,1},{1,0},{2,3},{3,2},{4,5},{5,4},{6,7},{7,6},{8,9},{9,8},{10,11... | collective-permute-start | bytes 3145736 | tf_op jit(solution)/shard_map/ppermute | solution.py:384
  131.9 4.0 collective-permute-start.11
  133.9 26.0 %collective-permute-start.13 = (bf16[512,1024]{1,0:T(8,128)(2,1)S(1)}, bf16[512,1024]{1,0:T(8,128)(2,1)S(1)}, u32[]{:S(2)}, u32[]{:S(2)}) collective-permute-start(bf16[512,1024]{1,0:T(8,128)(2,1)S(1)} %add_convert_fusion.6), channel_id=1, source_target_pairs={{0,2},{1,3},{2,0},{3,1},{4,6},{5,7},{6,4},{7,5},{8,10},{9,11},{10,... | collective-permute-start | bytes 3145736 | tf_op jit(solution)/shard_map/ppermute | solution.py:387
  134.5 48.0 %collective-permute-start.16 = (bf16[512,1024]{1,0:T(8,128)(2,1)}, bf16[512,1024]{1,0:T(8,128)(2,1)}, u32[]{:S(2)}, u32[]{:S(2)}) collective-permute-start(bf16[512,1024]{1,0:T(8,128)(2,1)} %param.33), channel_id=1, source_target_pairs={{0,2},{1,3},{2,0},{3,1},{4,6},{5,7},{6,4},{7,5},{8,10},{9,11},{10,... | collective-permute-start | bytes 3145736 | tf_op jit(solution)/shard_map/ppermute | solution.py:387
  161.5 42.9 %collective-permute-start.14 = (bf16[512,1024]{1,0:T(8,128)(2,1)}, bf16[512,1024]{1,0:T(8,128)(2,1)}, u32[]{:S(2)}, u32[]{:S(2)}) collective-permute-start(bf16[512,1024]{1,0:T(8,128)(2,1)} %get-tuple-element.213), channel_id=1, source_target_pairs={{0,2},{1,3},{2,0},{3,1},{4,6},{5,7},{6,4},{7,5},{8,10},{9,11},{10,... | collective-permute-start | bytes 3145736 | tf_op jit(solution)/shard_map/ppermute | solution.py:387
  162.1 51.5 %collective-permute-start.19 = (bf16[512,1024]{1,0:T(8,128)(2,1)}, bf16[512,1024]{1,0:T(8,128)(2,1)}, u32[]{:S(2)}, u32[]{:S(2)}) collective-permute-start(bf16[512,1024]{1,0:T(8,128)(2,1)} %param.33), channel_id=1, source_target_pairs={{0,1},{1,0},{2,3},{3,2},{4,5},{5,4},{6,7},{7,6},{8,9},{9,8},{10,11... | collective-permute-start | bytes 3145736 | tf_op jit(solution)/shard_map/ppermute | solution.py:384
  166.2 38.1 %copy-start.11 = (bf16[512,1024]{1,0:T(8,128)(2,1)S(1)}, bf16[512,1024]{1,0:T(8,128)(2,1)}, u32[]{:S(2)}) copy-start(bf16[512,1024]{1,0:T(8,128)(2,1)} %copy-done.10) | copy-start | bytes 3145732
  166.2 38.1 %copy-start.13 = (bf16[512,1024]{1,0:T(8,128)(2,1)S(1)}, bf16[512,1024]{1,0:T(8,128)(2,1)}, u32[]{:S(2)}) copy-start(bf16[512,1024]{1,0:T(8,128)(2,1)} %copy-done.12) | copy-start | bytes 3145732
  182.4 34.7 %collective-permute-start.17 = (bf16[512,1024]{1,0:T(8,128)(2,1)}, bf16[512,1024]{1,0:T(8,128)(2,1)S(1)}, u32[]{:S(2)}, u32[]{:S(2)}) collective-permute-start(bf16[512,1024]{1,0:T(8,128)(2,1)} %collective-permute-done.16), channel_id=1, source_target_pairs={{0,1},{1,0},{2,3},{3,2},{4,5},{5,4},{6,7},{7,6},{8,9},{9,8},{10,11... | collective-permute-start | bytes 3145736 | tf_op jit(solution)/shard_map/ppermute | solution.py:384
  209.6 17.7 %collective-permute-start.18 = (bf16[512,1024]{1,0:T(8,128)(2,1)}, bf16[512,1024]{1,0:T(8,128)(2,1)}, u32[]{:S(2)}, u32[]{:S(2)}) collective-permute-start(bf16[512,1024]{1,0:T(8,128)(2,1)} %get-tuple-element.246.refs_0_), channel_id=1, source_target_pairs={{0,1},{1,0},{2,3},{3,2},{4,5},{5,4},{6,7},{7,6},{8,9},{9,8},{10,11... | collective-permute-start | bytes 3145736 | tf_op jit(solution)/shard_map/ppermute | solution.py:384
  213.5 28.3 %collective-permute-start.15 = (bf16[512,1024]{1,0:T(8,128)(2,1)S(1)}, bf16[512,1024]{1,0:T(8,128)(2,1)}, u32[]{:S(2)}, u32[]{:S(2)}) collective-permute-start(bf16[512,1024]{1,0:T(8,128)(2,1)S(1)} %get-tuple-element.247.refs_0_), channel_id=1, source_target_pairs={{0,1},{1,0},{2,3},{3,2},{4,5},{5,4},{6,7},{7,6},{8,9},{9,8},{10,11... | collective-permute-start | bytes 3145736 | tf_op jit(solution)/shard_map/ppermute | solution.py:384
  234.4 24.1 %collective-permute-start.23 = (bf16[512,1024]{1,0:T(8,128)(2,1)}, bf16[512,1024]{1,0:T(8,128)(2,1)}, u32[]{:S(2)}, u32[]{:S(2)}) collective-permute-start(bf16[512,1024]{1,0:T(8,128)(2,1)} %get-tuple-element.112), channel_id=1, source_target_pairs={{0,1},{1,0},{2,3},{3,2},{4,5},{5,4},{6,7},{7,6},{8,9},{9,8},{10,11... | collective-permute-start | bytes 3145736 | tf_op jit(solution)/shard_map/ppermute | solution.py:384
  249.3 11.6 %collective-permute-start.24 = (bf16[512,1024]{1,0:T(8,128)(2,1)}, bf16[512,1024]{1,0:T(8,128)(2,1)S(1)}, u32[]{:S(2)}, u32[]{:S(2)}) collective-permute-start(bf16[512,1024]{1,0:T(8,128)(2,1)} %get-tuple-element.114), channel_id=1, source_target_pairs={{0,1},{1,0},{2,3},{3,2},{4,5},{5,4},{6,7},{7,6},{8,9},{9,8},{10,11... | collective-permute-start | bytes 3145736 | tf_op jit(solution)/shard_map/ppermute | solution.py:384
  257.9 11.7 %collective-permute-start.21 = (bf16[512,1024]{1,0:T(8,128)(2,1)}, bf16[512,1024]{1,0:T(8,128)(2,1)S(1)}, u32[]{:S(2)}, u32[]{:S(2)}) collective-permute-start(bf16[512,1024]{1,0:T(8,128)(2,1)} %get-tuple-element.232), channel_id=1, source_target_pairs={{0,1},{1,0},{2,3},{3,2},{4,5},{5,4},{6,7},{7,6},{8,9},{9,8},{10,11... | collective-permute-start | bytes 3145736 | tf_op jit(solution)/shard_map/ppermute | solution.py:384
  258.3 56.9 %collective-permute-start.20 = (bf16[512,1024]{1,0:T(8,128)(2,1)}, bf16[512,1024]{1,0:T(8,128)(2,1)S(1)}, u32[]{:S(2)}, u32[]{:S(2)}) collective-permute-start(bf16[512,1024]{1,0:T(8,128)(2,1)} %get-tuple-element.231), channel_id=1, source_target_pairs={{0,1},{1,0},{2,3},{3,2},{4,5},{5,4},{6,7},{7,6},{8,9},{9,8},{10,11... | collective-permute-start | bytes 3145736 | tf_op jit(solution)/shard_map/ppermute | solution.py:384
  260.2 26.1 %collective-permute-start.27 = (bf16[512,1024]{1,0:T(8,128)(2,1)S(1)}, bf16[512,1024]{1,0:T(8,128)(2,1)S(1)}, u32[]{:S(2)}, u32[]{:S(2)}) collective-permute-start(bf16[512,1024]{1,0:T(8,128)(2,1)S(1)} %add_convert_fusion.3), channel_id=1, source_target_pairs={{0,2},{1,3},{2,0},{3,1},{4,6},{5,7},{6,4},{7,5},{8,10},{9,11},{10,... | collective-permute-start | bytes 3145736 | tf_op jit(solution)/shard_map/ppermute | solution.py:387
  261.3 47.4 %collective-permute-start.25 = (bf16[512,1024]{1,0:T(8,128)(2,1)S(1)}, bf16[512,1024]{1,0:T(8,128)(2,1)S(1)}, u32[]{:S(2)}, u32[]{:S(2)}) collective-permute-start(bf16[512,1024]{1,0:T(8,128)(2,1)S(1)} %add_convert_fusion.2), channel_id=1, source_target_pairs={{0,2},{1,3},{2,0},{3,1},{4,6},{5,7},{6,4},{7,5},{8,10},{9,11},{10,... | collective-permute-start | bytes 3145736 | tf_op jit(solution)/shard_map/ppermute | solution.py:387
  270.1 60.6 %collective-permute-start.22 = (bf16[512,1024]{1,0:T(8,128)(2,1)S(1)}, bf16[512,1024]{1,0:T(8,128)(2,1)S(1)}, u32[]{:S(2)}, u32[]{:S(2)}) collective-permute-start(bf16[512,1024]{1,0:T(8,128)(2,1)S(1)} %add_convert_fusion.5), channel_id=1, source_target_pairs={{0,2},{1,3},{2,0},{3,1},{4,6},{5,7},{6,4},{7,5},{8,10},{9,11},{10,... | collective-permute-start | bytes 3145736 | tf_op jit(solution)/shard_map/ppermute | solution.py:387
  315.1 27.7 %collective-permute-start.28 = (bf16[512,1024]{1,0:T(8,128)(2,1)S(1)}, bf16[512,1024]{1,0:T(8,128)(2,1)S(1)}, u32[]{:S(2)}, u32[]{:S(2)}) collective-permute-start(bf16[512,1024]{1,0:T(8,128)(2,1)S(1)} %add_convert_fusion.1.refs_0_), channel_id=1, source_target_pairs={{0,1},{1,0},{2,3},{3,2},{4,5},{5,4},{6,7},{7,6},{8,9},{9,8},{10,11... | collective-permute-start | bytes 3145736 | tf_op jit(solution)/shard_map/ppermute | solution.py:384
  335.6 7.2 %collective-permute-start.26 = (bf16[512,1024]{1,0:T(8,128)(2,1)S(1)}, bf16[512,1024]{1,0:T(8,128)(2,1)S(1)}, u32[]{:S(2)}, u32[]{:S(2)}) collective-permute-start(bf16[512,1024]{1,0:T(8,128)(2,1)S(1)} %get-tuple-element.210.refs_0_), channel_id=1, source_target_pairs={{0,1},{1,0},{2,3},{3,2},{4,5},{5,4},{6,7},{7,6},{8,9},{9,8},{10,11... | collective-permute-start | bytes 3145736 | tf_op jit(solution)/shard_map/ppermute | solution.py:384
  386.7 20.6 %collective-permute-start.29 = (bf16[512,256]{1,0:T(8,128)(2,1)S(1)}, bf16[512,256]{1,0:T(8,128)(2,1)S(1)}, u32[]{:S(2)}, u32[]{:S(2)}) collective-permute-start(bf16[512,256]{1,0:T(8,128)(2,1)S(1)} %get-tuple-element.204), channel_id=1, source_target_pairs={{4,0},{8,4},{12,8},{16,12},{20,16},{24,20},{28,24},{5,1},{9,5},{13... | collective-permute-start | bytes 786440 | tf_op jit(solution)/shard_map/ppermute | solution.py:391
  404.7 62.3 %collective-permute-start.32 = (bf16[512,256]{1,0:T(8,128)(2,1)}, bf16[512,256]{1,0:T(8,128)(2,1)}, u32[]{:S(2)}, u32[]{:S(2)}) collective-permute-start(bf16[512,256]{1,0:T(8,128)(2,1)} %get-tuple-element.138), channel_id=1, source_target_pairs={{4,0},{8,4},{12,8},{16,12},{20,16},{24,20},{28,24},{5,1},{9,5},{13... | collective-permute-start | bytes 786440 | tf_op jit(solution)/shard_map/ppermute | solution.py:391
  406.0 61.0 %collective-permute-start.33 = (bf16[512,256]{1,0:T(8,128)(2,1)}, bf16[512,256]{1,0:T(8,128)(2,1)}, u32[]{:S(2)}, u32[]{:S(2)}) collective-permute-start(bf16[512,256]{1,0:T(8,128)(2,1)} %get-tuple-element.139), channel_id=1, source_target_pairs={{4,0},{8,4},{12,8},{16,12},{20,16},{24,20},{28,24},{5,1},{9,5},{13... | collective-permute-start | bytes 786440 | tf_op jit(solution)/shard_map/ppermute | solution.py:391
  408.0 25.9 %collective-permute-start.30 = (bf16[512,256]{1,0:T(8,128)(2,1)S(1)}, bf16[512,256]{1,0:T(8,128)(2,1)S(1)}, u32[]{:S(2)}, u32[]{:S(2)}) collective-permute-start(bf16[512,256]{1,0:T(8,128)(2,1)S(1)} %add_convert_fusion.9), channel_id=1, source_target_pairs={{8,0},{12,4},{16,8},{20,12},{24,16},{28,20},{9,1},{13,5},{17,9},{2... | collective-permute-start | bytes 786440 | tf_op jit(solution)/shard_map/ppermute | solution.py:391
  435.4 30.0 %collective-permute-start.31 = (bf16[512,256]{1,0:T(8,128)(2,1)}, bf16[512,256]{1,0:T(8,128)(2,1)S(1)}, u32[]{:S(2)}, u32[]{:S(2)}) collective-permute-start(bf16[512,256]{1,0:T(8,128)(2,1)} %add_convert_fusion.8), channel_id=1, source_target_pairs={{16,0},{20,4},{24,8},{28,12},{17,1},{21,5},{25,9},{29,13},{18,2},{... | collective-permute-start | bytes 786440 | tf_op jit(solution)/shard_map/ppermute | solution.py:391
  485.4 18.4 %all-to-all-start = ((bf16[8,64,512]{2,1,0:T(8,128)(2,1)}), bf16[8,64,512]{2,1,0:T(8,128)(2,1)S(1)}, u32[]{:S(2)}, u32[]{:S(2)}) async-start(bf16[8,64,512]{2,1,0:T(8,128)(2,1)} %pad_maximum_fusion.2), calls=%async_computation | async-start | bytes 1048576 | tf_op jit(solution)/shard_map/all_to_all | solution.py:825
  492.2 17.2 %collective-permute-start.35 = (bf16[512,1024]{1,0:T(8,128)(2,1)}, bf16[512,1024]{1,0:T(8,128)(2,1)S(1)}, u32[]{:S(2)}, u32[]{:S(2)}) collective-permute-start(bf16[512,1024]{1,0:T(8,128)(2,1)} %get-tuple-element.230), channel_id=1, source_target_pairs={{0,1},{1,0},{2,3},{3,2},{4,5},{5,4},{6,7},{7,6},{8,9},{9,8},{10,11... | collective-permute-start | bytes 3145736 | tf_op jit(solution)/shard_map/ppermute | solution.py:384
  503.8 50.3 %all-to-all-start.1 = ((bf16[8,128,768]{1,2,0:T(8,128)(2,1)}), bf16[8,128,768]{1,2,0:T(8,128)(2,1)}, u32[]{:S(2)}, u32[]{:S(2)}) async-start(bf16[8,128,768]{1,2,0:T(8,128)(2,1)} %copy_bitcast_fusion), calls=%async_computation.1 | async-start | bytes 3145728 | tf_op jit(solution)/shard_map/all_to_all | solution.py:822
  508.2 1.2 collective-permute-start.37
  508.3 39.0 %collective-permute-start.34 = (bf16[512,1024]{1,0:T(8,128)(2,1)}, bf16[512,1024]{1,0:T(8,128)(2,1)}, u32[]{:S(2)}, u32[]{:S(2)}) collective-permute-start(bf16[512,1024]{1,0:T(8,128)(2,1)} %get-tuple-element.229), channel_id=1, source_target_pairs={{0,1},{1,0},{2,3},{3,2},{4,5},{5,4},{6,7},{7,6},{8,9},{9,8},{10,11... | collective-permute-start | bytes 3145736 | tf_op jit(solution)/shard_map/ppermute | solution.py:384
  509.5 4.7 collective-permute-start.38
  512.1 35.2 %collective-permute-start.36 = (bf16[512,1024]{1,0:T(8,128)(2,1)}, bf16[512,1024]{1,0:T(8,128)(2,1)}, u32[]{:S(2)}, u32[]{:S(2)}) collective-permute-start(bf16[512,1024]{1,0:T(8,128)(2,1)} %add_convert_fusion), channel_id=1, source_target_pairs={{0,2},{1,3},{2,0},{3,1},{4,6},{5,7},{6,4},{7,5},{8,10},{9,11},{10,... | collective-permute-start | bytes 3145736 | tf_op jit(solution)/shard_map/ppermute | solution.py:387
  514.1 6.1 %collective-permute-start.39 = (f32[26,128]{1,0:T(8,128)S(1)}, f32[26,128]{1,0:T(8,128)S(1)}, u32[]{:S(2)}, u32[]{:S(2)}) collective-permute-start(f32[26,128]{1,0:T(8,128)S(1)} %fusion.105), channel_id=1, source_target_pairs={{0,4},{4,0},{8,12},{12,8},{16,20},{20,16},{24,28},{28,24},{1,5},{5... | collective-permute-start | bytes 39944 | tf_op jit(solution)/shard_map/ppermute | solution.py:841
  520.3 13.4 %collective-permute-start.40 = (f32[26,128]{1,0:T(8,128)S(1)}, f32[26,128]{1,0:T(8,128)S(1)}, u32[]{:S(2)}, u32[]{:S(2)}) collective-permute-start(f32[26,128]{1,0:T(8,128)S(1)} %add.315), channel_id=1, source_target_pairs={{0,8},{4,12},{8,0},{12,4},{16,24},{20,28},{24,16},{28,20},{1,9},{5... | collective-permute-start | bytes 39944 | tf_op jit(solution)/shard_map/ppermute | solution.py:841
  533.6 11.6 %collective-permute-start.41 = (f32[26,128]{1,0:T(8,128)S(1)}, f32[26,128]{1,0:T(8,128)S(1)}, u32[]{:S(2)}, u32[]{:S(2)}) collective-permute-start(f32[26,128]{1,0:T(8,128)S(1)} %add.316), channel_id=1, source_target_pairs={{0,16},{4,20},{8,24},{12,28},{16,0},{20,4},{24,8},{28,12},{1,17},{... | collective-permute-start | bytes 39944 | tf_op jit(solution)/shard_map/ppermute | solution.py:841
  (55 other events, 600.9 us)
Sparse Core Ops, SparseCore 0:
  353.8 117.0 reduce-scatter.3
